TPU v7x, 32 devices: a whole 2x2x4 slice. The times are simulated.
32 devices in a mesh: lat: 4 (over y, x), lon: 8 (over z, core).
Axes of the slice: x: 2, y: 2, z: 4, core: 2. Of those that a mesh axis runs over, the one named last changes fastest.
Arguments:
- fine_field: bfloat16 [4, 48, 96, 512], P(None, 'lat', 'lon'), may hold values from -6 to 6
- offsets: int32 [4], replicated, may hold values from 1 to 11, as said below
- fine_prenorm: float32 [512], replicated, may hold values from 0.25 to 1.75
- fine_triple: bfloat16 [512, 1536], replicated, may hold values from -0.25 to 0.25
- fine_bias: float32 [16, 144, 144], replicated, may hold values from -160 to 160
- fine_output: bfloat16 [512, 512], replicated, may hold values from -0.25 to 0.25
- fine_midnorm: float32 [512], replicated, may hold values from 0.25 to 1.75
- fine_expand: bfloat16 [512, 2048], replicated, may hold values from -0.25 to 0.25
- fine_reduce: bfloat16 [2048, 512], replicated, may hold values from -0.125 to 0.125
- merge_gain: float32 [2048], replicated, may hold values from 0.25 to 1.75
- merge_weight: bfloat16 [2048, 1024], replicated, may hold values from -0.125 to 0.125
- coarse_prenorm: float32 [1024], replicated, may hold values from 0.25 to 1.75
- coarse_triple: bfloat16 [1024, 3072], P(None, 'lon'), may hold values from -0.1875 to 0.1875
- coarse_bias: float32 [32, 144, 144], P('lon'), may hold values from -160 to 160
- coarse_output: bfloat16 [1024, 1024], P('lon'), may hold values from -0.1875 to 0.1875
- coarse_midnorm: float32 [1024], replicated, may hold values from 0.25 to 1.75
- coarse_expand: bfloat16 [1024, 4096], P(None, 'lon'), may hold values from -0.1875 to 0.1875
- coarse_reduce: bfloat16 [4096, 1024], P('lon'), may hold values from -0.09375 to 0.09375
- upsample_weight: bfloat16 [1024, 2048], replicated, may hold values from -0.1875 to 0.1875
Outputs:
- blended: bfloat16 [4, 48, 96, 512], P(None, 'lat', 'lon')
- coarse_state: bfloat16 [4, 24, 48, 1024], P(None, 'lat', 'lon')
Inputs may be any that keep to these rules, and one draw needn't show every extreme that they name: `offsets`: entries 0 and 2 lie in 1 to 5, entries 1 and 3 in 1 to 11; in every draw entry 0 or entry 2 equals 5, and entry 1 or entry 3 equals 11.
All inputs are finite; a program needn't handle non-finite values.
Results may differ from a plain program's by a relative error of at most 0.024.
Values may be sent and summed in bfloat16 or wider, within the bound.
A program may use at most 128 MiB of HBM per device.

v0:
```python
import functools

import jax
import jax.numpy as jnp
from jax import lax
from jax.experimental import pallas as pl
from jax.experimental.pallas import tpu as pltpu
from jax.sharding import PartitionSpec as P

WD = 2
WL = 6
WW = 12
WT = 144
HALF = WL * WW

epsilon = 1e-05
masked_score = -1e30
BF = jnp.bfloat16
F32 = jnp.float32


def layer_norm(values, gain_vec):
    values = values.astype(F32)
    center = jnp.mean(values, axis=-1, keepdims=True)
    offset_vals = values - center
    spread = jnp.mean(offset_vals * offset_vals, axis=-1, keepdims=True)
    return (offset_vals * lax.rsqrt(spread + epsilon) * gain_vec).astype(BF)


def dot32(left, right):
    return jnp.dot(left, right, preferred_element_type=F32)


def pick(source_rows, table):
    columns = jnp.arange(table.shape[0], dtype=jnp.int32)
    chosen = (source_rows[:, None] == columns[None, :]).astype(BF)
    return dot32(chosen, table).astype(BF)


def moved(block, axes, deltas):
    sizes = [lax.axis_size(a) for a in axes]
    pairs = []
    if len(axes) == 1:
        n = sizes[0]
        pairs = [((i - deltas[0]) % n, i) for i in range(n)]
        return lax.ppermute(block, axes[0], pairs)
    n, m = sizes
    for i in range(n):
        for j in range(m):
            origin = ((i - deltas[0]) % n) * m + (j - deltas[1]) % m
            pairs.append((origin, i * m + j))
    return lax.ppermute(block, axes, pairs)


def attend(triples, heads_all, head_dim, bias_ref, place_mask, write):
    group = 4 if heads_all % 4 == 0 else heads_all
    lanes = group * head_dim
    width = 3 * lanes
    row_id = lax.broadcasted_iota(jnp.int32, (width, width), 0)
    col_id = lax.broadcasted_iota(jnp.int32, (width, width), 1)
    kind = col_id // lanes
    head = (col_id % lanes) // head_dim
    origin = head * (3 * head_dim) + kind * head_dim + col_id % head_dim
    order = (row_id == origin).astype(F32).astype(BF)
    lane = lax.broadcasted_iota(jnp.int32, (WT, lanes), 1) // head_dim
    for g in range(heads_all // group):
        part = dot32(triples[:, g * width : (g + 1) * width], order)
        queries = part[:, :lanes]
        keys_all = part[:, lanes : 2 * lanes].astype(BF)
        values = part[:, 2 * lanes :].astype(BF)
        total = None
        for h in range(group):
            mine = jnp.where(lane == h, queries, 0.0).astype(BF)
            scores = lax.dot_general(
                mine, keys_all, (((1,), (1,)), ((), ())), preferred_element_type=F32
            )
            scores = scores * head_dim ** (-0.5) + bias_ref[g * group + h] + place_mask
            top = jnp.max(scores, axis=-1, keepdims=True)
            lifted = jnp.exp(scores - top)
            weight_sum = jnp.sum(lifted, axis=-1, keepdims=True)
            mixed = dot32(lifted.astype(BF), values) / weight_sum
            mixed = jnp.where(lane == h, mixed, 0.0)
            total = mixed if total is None else total + mixed
        write(g * lanes, lanes, total.astype(BF))


def window_mask(limit):
    row = (lax.broadcasted_iota(jnp.int32, (WT, WT), 0) // WW) % WL
    col = (lax.broadcasted_iota(jnp.int32, (WT, WT), 1) // WW) % WL
    row_in = (row >= limit).astype(jnp.int32)
    col_in = (col >= limit).astype(jnp.int32)
    return jnp.where(row_in == col_in, 0.0, masked_score)


def attention_kernel(head_dim, heads_all, projected, limit_ref, x_ref, *refs):
    if projected:
        bias_ref, out_ref = refs
        triples = x_ref[...]
    else:
        gain_ref, weight_ref, bias_ref, out_ref = refs
        triples = dot32(layer_norm(x_ref[...], gain_ref[...]), weight_ref[...]).astype(BF)

    def write(start, size, value):
        out_ref[:, start : start + size] = value

    attend(
        triples,
        heads_all,
        head_dim,
        bias_ref,
        window_mask(limit_ref[pl.program_id(0)]),
        write,
    )


def whole_block(array):
    zeros = (0,) * array.ndim
    return pl.BlockSpec(array.shape, lambda i: zeros)


def rows_block(array, rows):
    return pl.BlockSpec((rows, array.shape[1]), lambda i: (i, 0))


def attention(limits, rows, bias_table, head_dim, gain_vec=None, weight=None):
    heads_all = bias_table.shape[0]
    count = rows.shape[0] // WT
    extra = [] if weight is None else [gain_vec[None], weight]
    extra = extra + [bias_table]
    wide = heads_all * head_dim
    return pl.pallas_call(
        functools.partial(attention_kernel, head_dim, heads_all, weight is None),
        out_shape=jax.ShapeDtypeStruct((rows.shape[0], wide), BF),
        grid=(count,),
        in_specs=[pl.BlockSpec(memory_space=pltpu.SMEM), rows_block(rows, WT)]
        + [whole_block(e) for e in extra],
        out_specs=pl.BlockSpec((WT, wide), lambda i: (i, 0)),
        compiler_params=pltpu.CompilerParams(vmem_limit_bytes=40 << 20),
    )(limits, rows, *extra)


def tail_kernel(m_ref, x_ref, wo_ref, g_ref, we_ref, wr_ref, out_ref):
    attended = (x_ref[...].astype(F32) + dot32(m_ref[...], wo_ref[...])).astype(BF)
    hidden = jax.nn.gelu(dot32(layer_norm(attended, g_ref[...]), we_ref[...])).astype(BF)
    out_ref[...] = (attended.astype(F32) + dot32(hidden, wr_ref[...])).astype(BF)


def fine_tail(mixed, field, w_out, gain_vec, w_expand, w_reduce, rows):
    gain_vec = gain_vec[None]
    return pl.pallas_call(
        tail_kernel,
        out_shape=jax.ShapeDtypeStruct(field.shape, BF),
        grid=(field.shape[0] // rows,),
        in_specs=[rows_block(mixed, rows), rows_block(field, rows)]
        + [whole_block(e) for e in (w_out, gain_vec, w_expand, w_reduce)],
        out_specs=rows_block(field, rows),
        compiler_params=pltpu.CompilerParams(vmem_limit_bytes=40 << 20),
    )(mixed, field, w_out, gain_vec, w_expand, w_reduce)


def feed_kernel(x_ref, g_ref, we_ref, wr_ref, out_ref):
    hidden = jax.nn.gelu(dot32(layer_norm(x_ref[...], g_ref[...]), we_ref[...])).astype(BF)
    out_ref[...] = dot32(hidden, wr_ref[...]).astype(BF)


def feed(rows_in, gain_vec, w_expand, w_reduce, rows):
    gain_vec = gain_vec[None]
    return pl.pallas_call(
        feed_kernel,
        out_shape=jax.ShapeDtypeStruct(rows_in.shape, BF),
        grid=(rows_in.shape[0] // rows,),
        in_specs=[rows_block(rows_in, rows)]
        + [whole_block(e) for e in (gain_vec, w_expand, w_reduce)],
        out_specs=rows_block(rows_in, rows),
        compiler_params=pltpu.CompilerParams(vmem_limit_bytes=40 << 20),
    )(rows_in, gain_vec, w_expand, w_reduce)


def norm_dot_kernel(x_ref, g_ref, w_ref, out_ref):
    out_ref[...] = dot32(layer_norm(x_ref[...], g_ref[...]), w_ref[...]).astype(BF)


def norm_dot(rows_in, gain_vec, weight, rows):
    gain_vec = gain_vec[None]
    return pl.pallas_call(
        norm_dot_kernel,
        out_shape=jax.ShapeDtypeStruct((rows_in.shape[0], weight.shape[1]), BF),
        grid=(rows_in.shape[0] // rows,),
        in_specs=[rows_block(rows_in, rows)] + [whole_block(e) for e in (gain_vec, weight)],
        out_specs=pl.BlockSpec((rows, weight.shape[1]), lambda i: (i, 0)),
        compiler_params=pltpu.CompilerParams(vmem_limit_bytes=40 << 20),
    )(rows_in, gain_vec, weight)


def window_cells(total, rows, cols):
    n = jnp.arange(total, dtype=jnp.int32)
    w, place = n // WT, n % WT
    wc = w % (cols // WW)
    wl = (w // (cols // WW)) % (rows // WL)
    pd = w // ((cols // WW) * (rows // WL))
    return (
        pd * WD + place // HALF,
        wl * WL + (place // WW) % WL,
        wc * WW + place % WW,
    )


def window_place(p, i, j, rows, cols):
    w = ((p // WD) * (rows // WL) + i // WL) * (cols // WW) + j // WW
    return w * WT + (p % WD) * HALF + (i % WL) * WW + j % WW


def body(
    fine_field,
    offsets,
    fine_prenorm,
    fine_triple,
    fine_bias,
    fine_output,
    fine_midnorm,
    fine_expand,
    fine_reduce,
    merge_gain,
    merge_weight,
    coarse_prenorm,
    coarse_triple,
    coarse_bias,
    coarse_output,
    coarse_midnorm,
    coarse_expand,
    coarse_reduce,
    upsample_weight,
):
    levels, lat_rows, lon_cols, channels = fine_field.shape
    lat_count = lax.axis_size("lat")
    group_count = lax.axis_size("lon")
    lat_index = lax.axis_index("lat")
    s0, s1, s2, s3 = offsets[0], offsets[1], offsets[2], offsets[3]
    halo = WL - 1
    full_output = lax.all_gather(coarse_output, "lon", axis=0, tiled=True)

    cells = levels * lat_rows * lon_cols
    field = fine_field.reshape(cells, channels)
    strip = fine_field[:, :halo].reshape(-1, channels)
    strip_rows = strip.shape[0]
    extended = jnp.concatenate(
        [
            field,
            moved(field, ("lon",), (-1,)),
            moved(strip, ("lat",), (-1,)),
            moved(strip, ("lat", "lon"), (-1, -1)),
        ],
        axis=0,
    )
    p, i, j = window_cells(cells, lat_rows, lon_cols)
    i, j = i + s0, j + s1
    below, beside = i >= lat_rows, j >= lon_cols
    jj = jnp.where(beside, j - lon_cols, j)
    here = (p * lat_rows + i) * lon_cols + jj + jnp.where(beside, cells, 0)
    there = (
        2 * cells
        + (p * halo + i - lat_rows) * lon_cols
        + jj
        + jnp.where(beside, strip_rows, 0)
    )
    framed = pick(jnp.where(below, there, here), extended)
    win_rows = (jnp.arange(cells // WT, dtype=jnp.int32) // (lon_cols // WW)) % (lat_rows // WL)
    limits = lat_rows * lat_count - s0 - lat_index * lat_rows - win_rows * WL
    head_dim = channels // fine_bias.shape[0]
    mixed = attention(limits, framed, fine_bias, head_dim, fine_prenorm, fine_triple)

    u = jnp.arange(strip_rows, dtype=jnp.int32)
    up = u // (halo * lon_cols)
    ui = (u // lon_cols) % halo + lat_rows - halo
    mixed_strip = pick(window_place(up, ui, u % lon_cols, lat_rows, lon_cols), mixed)
    returned = jnp.concatenate(
        [
            mixed,
            moved(mixed, ("lon",), (1,)),
            moved(mixed_strip, ("lat",), (1,)),
            moved(mixed_strip, ("lat", "lon"), (1, 1)),
        ],
        axis=0,
    )
    half_rows = lat_rows // 2
    half_cols = lon_cols // 2
    few = cells // 4
    n = jnp.arange(cells, dtype=jnp.int32)
    block, cell = n // few, n % few
    c = cell % half_cols
    p = (cell // half_cols) % levels
    i = (cell // (half_cols * levels)) * 2 + block % 2
    j = c * 2 + block // 2
    ordered = pick((p * lat_rows + i) * lon_cols + j, field)
    fi, fj = i - s0, j - s1
    west = fj < 0
    fj = jnp.where(west, fj + lon_cols, fj)
    here = window_place(p, jnp.maximum(fi, 0), fj, lat_rows, lon_cols) + jnp.where(west, cells, 0)
    there = (
        2 * cells
        + (p * halo + fi + halo) * lon_cols
        + fj
        + jnp.where(west, strip_rows, 0)
    )
    mixed = pick(jnp.where(fi < 0, there, here), returned)
    fine_state = fine_tail(
        mixed, ordered, fine_output, fine_midnorm, fine_expand, fine_reduce, few
    )
    merged = jnp.concatenate([fine_state[k * few : (k + 1) * few] for k in range(4)], axis=1)
    coarse_in = norm_dot(merged, merge_gain, merge_weight, few)

    wide = coarse_in.shape[1]
    band = few * group_count
    band_cols = half_cols * group_count
    band_cells = lax.all_gather(coarse_in, "lon", axis=0, tiled=True)
    triples = norm_dot(band_cells, coarse_prenorm, coarse_triple, few)
    triple_width = triples.shape[1]
    per_row = levels * half_cols
    strip2 = triples.reshape(group_count, few, triple_width)[:, : halo * per_row]
    strip2 = strip2.reshape(-1, triple_width)
    extended2 = jnp.concatenate([triples, moved(strip2, ("lat",), (-1,))], axis=0)
    p, r, col = window_cells(band, half_rows, band_cols)
    r = r + s2
    col = (col + s3) % band_cols
    owner, c = col // half_cols, col % half_cols
    here = owner * few + r * per_row + p * half_cols + c
    there = band + owner * (halo * per_row) + (r - half_rows) * per_row + p * half_cols + c
    framed2 = pick(jnp.where(r >= half_rows, there, here), extended2)
    win_rows2 = (jnp.arange(band // WT, dtype=jnp.int32) // (band_cols // WW)) % (half_rows // WL)
    limits2 = half_rows * lat_count - s2 - lat_index * half_rows - win_rows2 * WL
    head_dim2 = triple_width // (3 * coarse_bias.shape[0])
    mixed2 = attention(limits2, framed2, coarse_bias, head_dim2)
    returned2 = jnp.concatenate([mixed2, moved(mixed2, ("lat",), (1,))], axis=0)
    n = jnp.arange(band, dtype=jnp.int32)
    owner, cell = n // few, n % few
    c = cell % half_cols
    p = (cell // half_cols) % levels
    fr = cell // per_row - s2
    col = (owner * half_cols + c - s3 + band_cols) % band_cols
    north = fr < 0
    fr = jnp.where(north, fr + half_rows, fr)
    source = window_place(p, fr, col, half_rows, band_cols) + jnp.where(north, band, 0)
    mixed2 = pick(source, returned2)
    mixed_width = mixed2.shape[1]
    parts = lax.all_to_all(
        mixed2.reshape(group_count, few, mixed_width), "lon", split_axis=0, concat_axis=0, tiled=True
    )
    grouped = jnp.concatenate([parts[g] for g in range(group_count)], axis=1)
    coarse_mid = (coarse_in.astype(F32) + dot32(grouped, full_output)).astype(BF)
    mid_band = lax.all_gather(coarse_mid, "lon", axis=0, tiled=True)
    product = feed(mid_band, coarse_midnorm, coarse_expand, coarse_reduce, few)
    feed_sum = lax.psum_scatter(product, "lon", scatter_dimension=0, tiled=True).astype(F32)
    coarse_state = (coarse_mid.astype(F32) + feed_sum).astype(BF)
    expanded = dot32(coarse_state, upsample_weight)
    spread = jnp.concatenate(
        [expanded[:, k * channels : (k + 1) * channels] for k in range(4)], axis=0
    )
    blended = (fine_state.astype(F32) + spread).astype(BF)
    n = jnp.arange(cells, dtype=jnp.int32)
    p = n // (lat_rows * lon_cols)
    i = (n // lon_cols) % lat_rows
    j = n % lon_cols
    source = (
        ((j % 2) * 2 + i % 2) * few + (i // 2) * per_row + p * half_cols + j // 2
    )
    blended = pick(source, blended).reshape(fine_field.shape)
    n = jnp.arange(few, dtype=jnp.int32)
    p = n // (half_rows * half_cols)
    r = (n // half_cols) % half_rows
    state = pick(r * per_row + p * half_cols + n % half_cols, coarse_state)
    return (blended, state.reshape(levels, half_rows, half_cols, wide))


def solution(mesh):
    placed = (
        P(None, "lat", "lon", None),
        P(),
        P(),
        P(),
        P(),
        P(),
        P(),
        P(),
        P(),
        P(),
        P(),
        P(),
        P(None, "lon"),
        P("lon", None, None),
        P("lon", None),
        P(),
        P(None, "lon"),
        P("lon", None),
        P(),
    )
    return jax.shard_map(
        body,
        mesh=mesh,
        in_specs=placed,
        out_specs=(P(None, "lat", "lon", None), P(None, "lat", "lon", None)),
        check_vma=False,
    )
```

profile of v0, /device:TPU:0, one launch (start us, length us, event | category | flops | bytes accessed | tf_op | source)
XLA Modules:
  0.0 244.7 jit_solution(13837638812508482328)
XLA Ops:
  7.2 1.3 copy.23
  8.5 0.1 reshape.666
  8.6 4.6 %collective-permute-start = (bf16[576,512]{1,0:T(8,128)(2,1)S(1)}, bf16[576,512]{1,0:T(8,128)(2,1)S(1)}, u32[]{:S(2)}, u32[]{:S(2)}) collective-permute-start(bf16[576,512]{1,0:T(8,128)(2,1)S(1)} %reshape.666), channel_id=1, source_target_pairs={{1,0},{2,1},{3,2},{4,3},{5,4},{6,5},{7,6},{0,7},{9,8},{10,9},{11,1... | collective-permute-start | bytes 1769480 | tf_op jit(solution)/shard_map/ppermute | solution.py:46
  13.3 2.5 %collective-permute-start.1 = (bf16[240,512]{1,0:T(8,128)(2,1)S(1)}, bf16[240,512]{1,0:T(8,128)(2,1)S(1)}, u32[]{:S(2)}, u32[]{:S(2)}) collective-permute-start(bf16[240,512]{1,0:T(8,128)(2,1)S(1)} %reshape.667), channel_id=1, source_target_pairs={{8,0},{16,8},{24,16},{0,24},{9,1},{17,9},{25,17},{1,25},{10,2},{18... | collective-permute-start | bytes 737288 | tf_op jit(solution)/shard_map/ppermute | solution.py:46
  15.8 0.4 collective-permute-start.2
  16.2 0.7 fusion.225
  17.5 1.3 add_select_fusion.49
  18.9 1.3 fusion.142
  20.3 4.5 %collective-permute-done.1 = bf16[240,512]{1,0:T(8,128)(2,1)S(1)} collective-permute-done((bf16[240,512]{1,0:T(8,128)(2,1)S(1)}, bf16[240,512]{1,0:T(8,128)(2,1)S(1)}, u32[]{:S(2)}, u32[]{:S(2)}) %collective-permute-start.1) | collective-permute-done | bytes 245792 | tf_op jit(solution)/shard_map/ppermute | solution.py:46
  24.9 1.3 fusion.31.x_ref
  26.2 9.6 %shard_map.194 = bf16[576,512]{1,0:T(8,128)(2,1)S(1)} custom-call(s32[4]{0:T(128)S(1)} %fusion.217.limit_ref, bf16[576,512]{1,0:T(8,128)(2,1)S(1)} %fusion.31.x_ref, f32[1,512]{1,0:T(1,128)S(1)} %bitcast.53, bf16[512,1536]{1,0:T(8,128)(2,1)S(1)} %copy-done.6, f32[16,144,144]{2,1,0:T(8,128)S(1)} %copy-done.1), custom_call_target="tpu_custom_call" | custom-call | tf_op jit(solution)/shard_map/pallas_call | solution.py:131
  35.9 0.4 convolution_convert_fusion.1
  36.3 2.4 collective-permute-start.4
  38.7 0.8 collective-permute-start.5
  39.5 0.7 fusion.29.x_ref
  40.2 6.1 %collective-permute-done.4 = bf16[240,512]{1,0:T(8,128)(2,1)S(1)} collective-permute-done((bf16[240,512]{1,0:T(8,128)(2,1)S(1)}, bf16[240,512]{1,0:T(8,128)(2,1)S(1)}, u32[]{:S(2)}, u32[]{:S(2)}) %collective-permute-start.4) | collective-permute-done | bytes 245792 | tf_op jit(solution)/shard_map/ppermute | solution.py:46
  46.3 6.0 %collective-permute-done.5 = bf16[240,512]{1,0:T(8,128)(2,1)S(1)} collective-permute-done((bf16[240,512]{1,0:T(8,128)(2,1)S(1)}, bf16[240,512]{1,0:T(8,128)(2,1)S(1)}, u32[]{:S(2)}, u32[]{:S(2)}) %collective-permute-start.5) | collective-permute-done | bytes 245792 | tf_op jit(solution)/shard_map/ppermute | solution.py:52
  52.4 1.3 fusion.34.m_ref
  53.7 5.3 %shard_map.195 = bf16[576,512]{1,0:T(8,128)(2,1)S(1)} custom-call(bf16[576,512]{1,0:T(8,128)(2,1)S(1)} %fusion.34.m_ref, bf16[576,512]{1,0:T(8,128)(2,1)S(1)} %fusion.29.x_ref, bf16[512,512]{1,0:T(8,128)(2,1)S(1)} %copy-done.11, f32[1,512]{1,0:T(1,128)S(1)} %bitcast.54, bf16[512,2048]{1,0:T(8,128)(2,1)S(1)} %copy-done.4, bf16[2048,512]{1,0:T(8,128)(2,1)S(1)} %copy-done.5), custom_call_target="tpu_custom_call" | custom-call | tf_op jit(solution)/shard_map/pallas_call | solution.py:150
  59.1 0.6 copy-done.12
  59.7 1.8 shard_map.196
  61.5 30.4 %all-gather.4.cloned.1.call-done.x_ref = bf16[1152,1024]{1,0:T(8,128)(2,1)} async-done(((bf16[144,1024]{1,0:T(8,128)(2,1)}), bf16[1152,1024]{1,0:T(8,128)(2,1)}) %all-gather.4.cloned.1.call-update) | async-done | bytes 2359312 | tf_op jit(solution)/shard_map/all_gather | solution.py:315
  91.9 1.7 copy-done.2
  93.6 4.1 %shard_map.197 = bf16[1152,384]{1,0:T(8,128)(2,1)S(1)} custom-call(bf16[1152,1024]{1,0:T(8,128)(2,1)S(1)} %copy-done.2, f32[1,1024]{1,0:T(1,128)S(1)} %bitcast.51, bf16[1024,384]{1,0:T(8,128)(2,1)S(1)} %copy-done.9), custom_call_target="tpu_custom_call" | custom-call | tf_op jit(solution)/shard_map/pallas_call | solution.py:185
  97.8 2.4 collective-permute-start.6
  100.2 0.2 all-gather.8.cloned.1.call-start
  101.0 1.3 add_select_fusion.23
  102.4 14.1 %collective-permute-done.6 = bf16[960,384]{1,0:T(8,128)(2,1)S(1)} collective-permute-done((bf16[960,384]{1,0:T(8,128)(2,1)S(1)}, bf16[960,384]{1,0:T(8,128)(2,1)S(1)}, u32[]{:S(2)}, u32[]{:S(2)}) %collective-permute-start.6) | collective-permute-done | bytes 737312 | tf_op jit(solution)/shard_map/ppermute | solution.py:46
  116.4 2.9 %fusion.6.x_ref = bf16[1152,384]{1,0:T(8,128)(2,1)S(1)} fusion(s32[1152]{0:T(1024)S(1)} %add_select_fusion.23, bf16[960,384]{1,0:T(8,128)(2,1)S(1)} %collective-permute-done.6, bf16[1152,384]{1,0:T(8,128)(2,1)S(1)} %shard_map.197), kind=kOutput, calls=%fused_computation.10 | convolution fusion | flops 1874681856 | bytes 2511360 | tf_op jit(solution)/shard_map/dot_general | solution.py:31
  119.4 6.6 %shard_map.198 = bf16[1152,128]{1,0:T(8,128)(2,1)S(1)} custom-call(s32[8]{0:T(128)S(1)} %sub.298.limit_ref, bf16[1152,384]{1,0:T(8,128)(2,1)S(1)} %fusion.6.x_ref, f32[4,144,144]{2,1,0:T(8,128)S(1)} %copy-done.10), custom_call_target="tpu_custom_call" | custom-call | tf_op jit(solution)/shard_map/pallas_call | solution.py:131
  125.9 2.4 collective-permute-start.7
  128.3 1.3 fusion.64
  129.7 6.2 %collective-permute-done.7 = bf16[1152,128]{1,0:T(8,128)(2,1)S(1)} collective-permute-done((bf16[1152,128]{1,0:T(8,128)(2,1)S(1)}, bf16[1152,128]{1,0:T(8,128)(2,1)S(1)}, u32[]{:S(2)}, u32[]{:S(2)}) %collective-permute-start.7) | collective-permute-done | bytes 294944 | tf_op jit(solution)/shard_map/ppermute | solution.py:46
  135.9 1.9 fusion.7
  137.8 13.2 %all_to_all.5 = bf16[8,144,128]{2,1,0:T(8,128)(2,1)S(1)} all-to-all(bf16[8,144,128]{2,1,0:T(8,128)(2,1)S(1)} %bitcast.56), channel_id=1, replica_groups=mesh['lat'=4,'lon'=8] {'lon'}, dimensions={0} | all-to-all | bytes 589824 | tf_op jit(solution)/shard_map/all_to_all | solution.py:345
  151.2 2.9 %fusion.37 = bf16[144,1024]{1,0:T(8,128)(2,1)} fusion(bf16[144,1024]{1,0:T(8,128)(2,1)S(1)} %fusion.48, bf16[1024,1024]{1,0:T(8,128)(2,1)} %all-gather.6.cloned.1.call-done, bf16[144,1024]{1,0:T(8,128)(2,1)} %shard_map.196), kind=kOutput, calls=%fused_computation.41 | convolution fusion | flops 302432256 | bytes 2981888 | tf_op jit(solution)/shard_map/dot_general | solution.py:31
  154.1 29.8 %all-gather.8.cloned.1.call-done.x_ref = bf16[1152,1024]{1,0:T(8,128)(2,1)} async-done(((bf16[144,1024]{1,0:T(8,128)(2,1)}), bf16[1152,1024]{1,0:T(8,128)(2,1)}) %all-gather.8.cloned.1.call-update) | async-done | bytes 2359312 | tf_op jit(solution)/shard_map/all_gather | solution.py:350
  183.9 1.7 copy-done.3
  185.6 1.2 copy-done.8
  186.8 7.4 %shard_map.199 = bf16[1152,1024]{1,0:T(8,128)(2,1)} custom-call(bf16[1152,1024]{1,0:T(8,128)(2,1)S(1)} %copy-done.3, f32[1,1024]{1,0:T(1,128)S(1)} %bitcast.52, bf16[1024,512]{1,0:T(8,128)(2,1)S(1)} %copy-done.7, bf16[512,1024]{1,0:T(8,128)(2,1)S(1)} %copy-done.8), custom_call_target="tpu_custom_call" | custom-call | tf_op jit(solution)/shard_map/pallas_call | solution.py:168
  194.2 36.4 %reduce-scatter.2.cloned.1.call-done = bf16[144,1024]{1,0:T(8,128)(2,1)} async-done(((bf16[1152,1024]{1,0:T(8,128)(2,1)}), bf16[144,1024]{1,0:T(8,128)(2,1)}) %reduce-scatter.2.cloned.1.call-update) | async-done | bytes 294928 | tf_op jit(solution)/shard_map/reduce_scatter | solution.py:352
  230.6 1.3 convolution_convert_fusion
  231.9 0.1 reshape.672
  232.1 0.9 copy.26
  233.0 3.0 %fusion.46 = f32[144,2048]{1,0:T(8,128)S(1)} fusion(bf16[1024,2048]{1,0:T(8,128)(2,1)} %param.37, bf16[144,1024]{1,0:T(8,128)(2,1)S(1)} %copy-done.18, bf16[144,1024]{1,0:T(8,128)(2,1)S(1)} %copy-done.17), kind=kOutput, calls=%fused_computation.55 | convolution fusion | flops 604569600 | bytes 5963776 | tf_op jit(solution)/shard_map/dot_general | solution.py:31
  236.1 0.7 fusion.30
  236.8 0.1 reshape.671
  236.9 1.3 copy.25
  (70 shorter events, 1.0 us)
Async XLA Ops:
  7.2 6.1 %slice-start = ((bf16[4,12,12,512]{3,0,2,1:T(4,128)(2,1)}), bf16[4,5,12,512]{3,0,2,1:T(4,128)(2,1)S(1)}, s32[]{:S(2)}) async-start(bf16[4,12,12,512]{3,0,2,1:T(4,128)(2,1)} %param.19), calls=%async_computation.6 | async-start | bytes 491520 | tf_op jit(solution)/shard_map/slice | solution.py:244
  7.2 84.8 %all-gather.4.cloned.1.call-start = ((), (), s32[]{:S(2)}) async-start(), calls=%async_computation.2 | async-start | bytes 2654208 | tf_op jit(solution)/shard_map/all_gather | solution.py:315
  8.5 7.7 %copy-start.19 = (s32[4]{0:T(128)S(1)}, s32[4]{0:T(128)}, u32[]{:S(2)}) copy-start(s32[4]{0:T(128)} %param.20) | copy-start | bytes 52
  8.6 16.2 %collective-permute-start = (bf16[576,512]{1,0:T(8,128)(2,1)S(1)}, bf16[576,512]{1,0:T(8,128)(2,1)S(1)}, u32[]{:S(2)}, u32[]{:S(2)}) collective-permute-start(bf16[576,512]{1,0:T(8,128)(2,1)S(1)} %reshape.666), channel_id=1, source_target_pairs={{1,0},{2,1},{3,2},{4,3},{5,4},{6,5},{7,6},{0,7},{9,8},{10,9},{11,1... | collective-permute-start | bytes 1769480 | tf_op jit(solution)/shard_map/ppermute | solution.py:46
  13.3 11.5 %collective-permute-start.1 = (bf16[240,512]{1,0:T(8,128)(2,1)S(1)}, bf16[240,512]{1,0:T(8,128)(2,1)S(1)}, u32[]{:S(2)}, u32[]{:S(2)}) collective-permute-start(bf16[240,512]{1,0:T(8,128)(2,1)S(1)} %reshape.667), channel_id=1, source_target_pairs={{8,0},{16,8},{24,16},{0,24},{9,1},{17,9},{25,17},{1,25},{10,2},{18... | collective-permute-start | bytes 737288 | tf_op jit(solution)/shard_map/ppermute | solution.py:46
  15.8 9.0 %collective-permute-start.2 = (bf16[240,512]{1,0:T(8,128)(2,1)S(1)}, bf16[240,512]{1,0:T(8,128)(2,1)S(1)}, u32[]{:S(2)}, u32[]{:S(2)}) collective-permute-start(bf16[240,512]{1,0:T(8,128)(2,1)S(1)} %reshape.667), channel_id=1, source_target_pairs={{9,0},{10,1},{11,2},{12,3},{13,4},{14,5},{15,6},{8,7},{17,8},{18,9... | collective-permute-start | bytes 737288 | tf_op jit(solution)/shard_map/ppermute | solution.py:52
  20.3 5.9 %copy-start.1 = (f32[16,144,144]{2,1,0:T(8,128)S(1)}, f32[16,144,144]{2,1,0:T(8,128)}, u32[]{:S(2)}) copy-start(f32[16,144,144]{2,1,0:T(8,128)} %refs_2_.1) | copy-start | bytes 3981316
  20.3 5.9 %copy-start.6 = (bf16[512,1536]{1,0:T(8,128)(2,1)S(1)}, bf16[512,1536]{1,0:T(8,128)(2,1)}, u32[]{:S(2)}) copy-start(bf16[512,1536]{1,0:T(8,128)(2,1)} %refs_1_.1) | copy-start | bytes 4718596
  20.3 5.9 %copy-start.15 = (f32[512]{0:T(512)S(1)}, f32[512]{0:T(512)}, u32[]{:S(2)}) copy-start(f32[512]{0:T(512)} %param.21) | copy-start | bytes 6148
  35.8 16.5 %collective-permute-start.3 = (bf16[576,512]{1,0:T(8,128)(2,1)S(1)}, bf16[576,512]{1,0:T(8,128)(2,1)S(1)}, u32[]{:S(2)}, u32[]{:S(2)}) collective-permute-start(bf16[576,512]{1,0:T(8,128)(2,1)S(1)} %shard_map.194), channel_id=1, source_target_pairs={{7,0},{0,1},{1,2},{2,3},{3,4},{4,5},{5,6},{6,7},{15,8},{8,9},{9,10... | collective-permute-start | bytes 1769480 | tf_op jit(solution)/shard_map/ppermute | solution.py:46
  36.3 10.0 %collective-permute-start.4 = (bf16[240,512]{1,0:T(8,128)(2,1)S(1)}, bf16[240,512]{1,0:T(8,128)(2,1)S(1)}, u32[]{:S(2)}, u32[]{:S(2)}) collective-permute-start(bf16[240,512]{1,0:T(8,128)(2,1)S(1)} %convolution_convert_fusion.1), channel_id=1, source_target_pairs={{24,0},{0,8},{8,16},{16,24},{25,1},{1,9},{9,17},{17,25},{26,2},{2,... | collective-permute-start | bytes 737288 | tf_op jit(solution)/shard_map/ppermute | solution.py:46
  38.7 13.6 %collective-permute-start.5 = (bf16[240,512]{1,0:T(8,128)(2,1)S(1)}, bf16[240,512]{1,0:T(8,128)(2,1)S(1)}, u32[]{:S(2)}, u32[]{:S(2)}) collective-permute-start(bf16[240,512]{1,0:T(8,128)(2,1)S(1)} %convolution_convert_fusion.1), channel_id=1, source_target_pairs={{31,0},{24,1},{25,2},{26,3},{27,4},{28,5},{29,6},{30,7},{7,8},{0,9... | collective-permute-start | bytes 737288 | tf_op jit(solution)/shard_map/ppermute | solution.py:52
  40.2 13.5 %copy-start.4 = (bf16[512,2048]{1,0:T(8,128)(2,1)S(1)}, bf16[512,2048]{1,0:T(8,128)(2,1)}, u32[]{:S(2)}) copy-start(bf16[512,2048]{1,0:T(8,128)(2,1)} %we_ref.2) | copy-start | bytes 6291460
  40.2 13.5 %copy-start.5 = (bf16[2048,512]{1,0:T(8,128)(2,1)S(1)}, bf16[2048,512]{1,0:T(8,128)(2,1)}, u32[]{:S(2)}) copy-start(bf16[2048,512]{1,0:T(8,128)(2,1)} %wr_ref.2) | copy-start | bytes 6291460
  40.2 13.5 %copy-start.11 = (bf16[512,512]{1,0:T(8,128)(2,1)S(1)}, bf16[512,512]{1,0:T(8,128)(2,1)}, u32[]{:S(2)}) copy-start(bf16[512,512]{1,0:T(8,128)(2,1)} %wo_ref.1) | copy-start | bytes 1572868
  40.2 13.5 %copy-start.16 = (f32[512]{0:T(512)S(1)}, f32[512]{0:T(512)}, u32[]{:S(2)}) copy-start(f32[512]{0:T(512)} %param.25) | copy-start | bytes 6148
  53.7 5.4 %copy-start = (bf16[2048,1024]{1,0:T(8,128)(2,1)S(1)}, bf16[2048,1024]{1,0:T(8,128)(2,1)}, u32[]{:S(2)}) copy-start(bf16[2048,1024]{1,0:T(8,128)(2,1)} %w_ref.2) | copy-start | bytes 12582916
  59.0 0.7 copy-start.12
  59.7 32.3 %copy-start.9 = (bf16[1024,384]{1,0:T(8,128)(2,1)S(1)}, bf16[1024,384]{1,0:T(8,128)(2,1)}, u32[]{:S(2)}) copy-start(bf16[1024,384]{1,0:T(8,128)(2,1)} %w_ref.3) | copy-start | bytes 2359300
  59.7 32.3 %copy-start.13 = (f32[1024]{0:T(1024)S(1)}, f32[1024]{0:T(1024)}, u32[]{:S(2)}) copy-start(f32[1024]{0:T(1024)} %param.30) | copy-start | bytes 12292
  61.5 89.7 %all-gather.6.cloned.1.call-start = ((), (), s32[]{:S(2)}) async-start(), calls=%async_computation.3 | async-start | bytes 2359296 | tf_op jit(solution)/shard_map/all_gather | solution.py:240
  91.9 1.7 copy-start.2
  97.8 18.7 %collective-permute-start.6 = (bf16[960,384]{1,0:T(8,128)(2,1)S(1)}, bf16[960,384]{1,0:T(8,128)(2,1)S(1)}, u32[]{:S(2)}, u32[]{:S(2)}) collective-permute-start(bf16[960,384]{1,0:T(8,128)(2,1)S(1)} %bitcast.55), channel_id=1, source_target_pairs={{8,0},{16,8},{24,16},{0,24},{9,1},{17,9},{25,17},{1,25},{10,2},{18... | collective-permute-start | bytes 2211848 | tf_op jit(solution)/shard_map/ppermute | solution.py:46
  100.2 83.7 %all-gather.8.cloned.1.call-start = ((), (), s32[]{:S(2)}) async-start(), calls=%async_computation.4 | async-start | bytes 2654208 | tf_op jit(solution)/shard_map/all_gather | solution.py:350
  102.3 17.0 %copy-start.10 = (f32[4,144,144]{2,1,0:T(8,128)S(1)}, f32[4,144,144]{2,1,0:T(8,128)}, u32[]{:S(2)}) copy-start(f32[4,144,144]{2,1,0:T(8,128)} %refs_0_.1) | copy-start | bytes 995332
  125.9 10.0 %collective-permute-start.7 = (bf16[1152,128]{1,0:T(8,128)(2,1)S(1)}, bf16[1152,128]{1,0:T(8,128)(2,1)S(1)}, u32[]{:S(2)}, u32[]{:S(2)}) collective-permute-start(bf16[1152,128]{1,0:T(8,128)(2,1)S(1)} %shard_map.198), channel_id=1, source_target_pairs={{24,0},{0,8},{8,16},{16,24},{25,1},{1,9},{9,17},{17,25},{26,2},{2,... | collective-permute-start | bytes 884744 | tf_op jit(solution)/shard_map/ppermute | solution.py:46
  151.1 32.8 %copy-start.7 = (bf16[1024,512]{1,0:T(8,128)(2,1)S(1)}, bf16[1024,512]{1,0:T(8,128)(2,1)}, u32[]{:S(2)}) copy-start(bf16[1024,512]{1,0:T(8,128)(2,1)} %we_ref.3) | copy-start | bytes 3145732
  151.1 32.8 %copy-start.14 = (f32[1024]{0:T(1024)S(1)}, f32[1024]{0:T(1024)}, u32[]{:S(2)}) copy-start(f32[1024]{0:T(1024)} %param.34) | copy-start | bytes 12292
  154.1 76.5 %reduce-scatter.2.cloned.1.call-start = ((), (), s32[]{:S(2)}) async-start(), calls=%async_computation.5 | async-start | bytes 2654208 | tf_op jit(solution)/shard_map/reduce_scatter | solution.py:352
  183.9 1.7 copy-start.3
  185.6 1.2 copy-start.8
  194.2 36.5 %copy-start.17 = (bf16[144,1024]{1,0:T(8,128)(2,1)S(1)}, bf16[144,1024]{1,0:T(8,128)(2,1)}, u32[]{:S(2)}) copy-start(bf16[144,1024]{1,0:T(8,128)(2,1)} %fusion.37) | copy-start | bytes 884740
  230.6 2.4 copy-start.18
Sparse Core Ops, SparseCore 0:
  61.6 30.2 all-gather.3
  100.3 26.5 all-gather.5
  154.2 29.6 all-gather.7
  194.3 36.2 reduce-scatter.1
where the time goes:
time: 245 us
  waiting for transfers between devices  134 us (55%)
  Pallas kernels  34.7 us (14%)
  matrix products  16.3 us (7%)
  starting transfers between devices  15.9 us (6%)
  between operations  15.5 us (6%)
  blocking collectives  13.2 us (5%)
  local copies, waits for them, and re-layouts  10.2 us (4%)
  other arithmetic  5.49 us (2%)
    reduce_scatter x1, waiting for transfers between devices, body(): lax.psum_scatter(product, 'lon', scatter_dimension=0, tiled=True)  36.4 us
    ppermute x6, waiting for transfers between devices, moved(): return lax.ppermute(block, axes[0], pairs)  30.9 us
    all_gather x1, waiting for transfers between devices, body(): band_cells = lax.all_gather(coarse_in, 'lon', axis=0, tiled=True)  30.4 us
    all_gather x1, waiting for transfers between devices, body(): mid_band = lax.all_gather(coarse_mid, 'lon', axis=0, tiled=True)  29.8 us
    dot_general x10, matrix products, dot32(): return jnp.dot(left, right, preferred_element_type=F32)  16.3 us
    pallas_call x2, Pallas kernels, attention(): pl.pallas_call(functools.partial(attention_kernel, head_dim, heads_all, w...  16.2 us
    ppermute x6, starting transfers between devices, moved(): return lax.ppermute(block, axes[0], pairs)  14.4 us
    all_to_all x1, blocking collectives, body(): lax.all_to_all(mixed2.reshape(group_count, few, mixed_width), 'lon', spli...  13.2 us
  transfers between devices with their start and end apart: 12, of which 8 were waited for; matrix products, arithmetic and copies ran while one was open for 5% of the time, Pallas kernels for 3%

commit v1 on v0

v1 whole, which is shorter than its diff:
```python
import functools

import jax
import jax.numpy as jnp
from jax import lax
from jax.experimental import pallas as pl
from jax.experimental.pallas import tpu as pltpu
from jax.sharding import PartitionSpec as P

WD = 2
WL = 6
WW = 12
WT = 144
HALO = WL - 1

epsilon = 1e-05
masked_score = -1e30
BF = jnp.bfloat16
F32 = jnp.float32
I32 = jnp.int32
MESH = pl.DeviceIdType.MESH


def up_to(value, step):
    return -(-value // step) * step


def layer_norm(values, gain_vec):
    values = values.astype(F32)
    center = jnp.mean(values, axis=-1, keepdims=True)
    offset_vals = values - center
    spread = jnp.mean(offset_vals * offset_vals, axis=-1, keepdims=True)
    return (offset_vals * lax.rsqrt(spread + epsilon) * gain_vec).astype(BF)


def dot32(left, right):
    return jnp.dot(left, right, preferred_element_type=F32)


def down(count):
    return lax.broadcasted_iota(I32, (count, 1), 0)


def along(count):
    return lax.broadcasted_iota(I32, (1, count), 1)


def one_hot(row_key, col_key):
    return (row_key == col_key).astype(F32).astype(BF)


def flat(block):
    return block.astype(F32).reshape(-1, block.shape[-1]).astype(BF)


def window_mask(limit):
    row = (lax.broadcasted_iota(I32, (WT, WT), 0) // WW) % WL
    col = (lax.broadcasted_iota(I32, (WT, WT), 1) // WW) % WL
    row_in = (row >= limit).astype(I32)
    col_in = (col >= limit).astype(I32)
    return jnp.where(row_in == col_in, 0.0, masked_score)


def head_order(heads, head_dim):
    lanes = heads * head_dim
    width = 3 * lanes
    row = down(width)
    col = along(width)
    origin = ((col % lanes) // head_dim) * (3 * head_dim) + (col // lanes) * head_dim + col % head_dim
    return one_hot(row, origin)


def attend(part, heads, head_dim, bias_at, place_mask):
    lanes = heads * head_dim
    queries = part[:, :lanes].astype(F32)
    keys_all = part[:, lanes : 2 * lanes].astype(BF)
    values = part[:, 2 * lanes :].astype(BF)
    lane = lax.broadcasted_iota(I32, (WT, lanes), 1) // head_dim
    total = None
    for h in range(heads):
        mine = jnp.where(lane == h, queries, 0.0).astype(BF)
        scores = lax.dot_general(
            mine, keys_all, (((1,), (1,)), ((), ())), preferred_element_type=F32
        )
        scores = scores * head_dim ** (-0.5) + bias_at(h) + place_mask
        top = jnp.max(scores, axis=-1, keepdims=True)
        lifted = jnp.exp(scores - top)
        weight_sum = jnp.sum(lifted, axis=-1, keepdims=True)
        mixed = dot32(lifted.astype(BF), values) / weight_sum
        mixed = jnp.where(lane == h, mixed, 0.0)
        total = mixed if total is None else total + mixed
    return total


class Copies:
    def __init__(self, send, recv, make):
        self.send, self.recv, self.make = send, recv, make

    def one(self, *index):
        src, dst, device = self.make(*index)
        return pltpu.make_async_remote_copy(
            src, dst, self.send.at[index], self.recv.at[index], device_id=device, device_id_type=MESH
        )


def step_kernel(cfg, names, *refs):
    r = dict(zip(names, refs))
    m, n, nz = cfg["m"], cfg["n"], cfg["n"] // 2
    pds, rows, cols = cfg["pds"], cfg["rows"], cfg["cols"]
    seg = WD * cols
    cells = rows * seg
    half = rows // 2
    hc = cols // 2
    per_row = WD * hc
    few = half * per_row
    fewp = up_to(few, 16)
    hal = up_to(HALO * per_row, 16)
    heads1, heads2, hd = cfg["heads1"], cfg["heads2"], cfg["hd"]
    lanes2 = heads2 * hd
    wins = rows // WL
    lat = lax.axis_index("lat")
    lon = lax.axis_index("lon")
    zi, core = lon // 2, lon % 2
    buddy = lon + 1 - 2 * core
    s0, s1, s2, s3 = r["off"][0], r["off"][1], r["off"][2], r["off"][3]

    def dev(dlat, dlon):
        return (lax.rem(lat + dlat + m, m), lax.rem(lon + dlon + n, n))

    greet = {(0, d) for d in range(1, n)}
    greet |= {(d % m, e) for d in (-1, 1) for e in range(n)}
    greet |= {(d, 0) for d in range(1, m)}
    greet -= {(0, 0)}
    barrier = pltpu.get_barrier_semaphore()
    for dlat, dlon in sorted(greet):
        pl.semaphore_signal(barrier, 1, device_id=dev(dlat, dlon), device_id_type=MESH)

    def local(k, src, dst):
        return pltpu.make_async_copy(src, dst, r["lsem"].at[k])

    E = [r["E%d" % pd] for pd in range(pds)]
    G = [r["G%d" % pd] for pd in range(pds)]
    loads = {
        "x0": local(0, r["x"].at[0], E[0].at[0, pl.ds(0, rows)]),
        "x1": local(1, r["x"].at[1], E[1].at[0, pl.ds(0, rows)]),
        "wt": local(2, r["wt"], r["v_wt"]),
        "b1": local(3, r["b1"], r["v_b1"]),
        "wo1": local(4, r["wo1"], r["v_wo1"]),
        "we1": local(5, r["we1"], r["v_we1"]),
        "wr1": local(6, r["wr1"], r["v_wr1"]),
        "mw": local(7, r["mw"], r["v_mw"]),
        "wt2": local(8, r["wt2"], r["v_wt2"].at[core]),
        "b2": local(9, r["b2"], r["v_b2"]),
        "we2": local(10, r["we2"], r["v_we2"].at[core]),
        "wr2": local(11, r["wr2"], r["v_wr2"].at[core]),
        "up": local(12, r["up"], r["v_up"]),
        "wo2": local(13, r["wo2"].at[lat], r["W"].at[core, lat, zi]),
    }
    for key in ("x0", "x1", "wt", "b1", "wo2"):
        loads[key].start()

    halo_copies = [
        Copies(r["hs%d" % k], r["hr%d" % k], make)
        for k, make in enumerate(
            (
                lambda pd: (r["x"].at[pd], E[pd].at[1, pl.ds(0, rows)], dev(0, -1)),
                lambda pd: (r["x"].at[pd, pl.ds(0, HALO)], E[pd].at[0, pl.ds(rows, HALO)], dev(-1, 0)),
                lambda pd: (r["x"].at[pd, pl.ds(0, HALO)], E[pd].at[1, pl.ds(rows, HALO)], dev(-1, -1)),
            )
        )
    ]
    low = rows - HALO
    back_copies = [
        Copies(r["bs%d" % k], r["br%d" % k], make)
        for k, make in enumerate(
            (
                lambda pd: (G[pd].at[0, pl.ds(HALO, rows)], G[pd].at[1, pl.ds(HALO, rows)], dev(0, 1)),
                lambda pd: (G[pd].at[0, pl.ds(HALO + low, HALO)], G[pd].at[0, pl.ds(0, HALO)], dev(1, 0)),
                lambda pd: (G[pd].at[0, pl.ds(HALO + low, HALO)], G[pd].at[1, pl.ds(0, HALO)], dev(1, 1)),
            )
        )
    ]
    W = r["W"]
    share_lon = Copies(
        r["ws0"], r["wr0"], lambda k: (r["wo2"].at[lat], W.at[core, lat, zi], dev(0, 2 * (k + 1)))
    )
    share_lat = Copies(r["ws1"], r["wr1s"], lambda k: (W.at[core, lat], W.at[core, lat], dev(k + 1, 0)))
    share_core = Copies(r["ws2"], r["wr2s"], lambda k: (W.at[core], W.at[core], (lat, buddy)))

    def swap(k):
        name = ("wt2", "we2", "wr2")[k]
        return pltpu.make_async_remote_copy(
            r[name],
            r["v_" + name].at[core],
            r["ss"].at[k],
            r["sr"].at[k],
            device_id=(lat, buddy),
            device_id_type=MESH,
        )

    X, Y, S, H = r["X"], r["Y"], r["S"], r["H"]
    gather1 = Copies(
        r["as0"], r["ar0"], lambda pd, k: (X.at[pd, zi], X.at[pd, zi], dev(0, 2 * (k + 1)))
    )
    cross = [
        Copies(r["cs%d" % k], r["cr%d" % k], make)
        for k, make in enumerate(
            (
                lambda pd: (S.at[pd], Y.at[pd, core], (lat, buddy)),
                lambda pd: (Y.at[pd, core, :, pl.ds(0, hal)], H.at[pd, core], dev(-1, 0)),
                lambda pd: (S.at[pd, :, pl.ds(0, hal)], H.at[pd, core], (lax.rem(lat + m - 1, m), buddy)),
            )
        )
    ]
    C, D, M, N = r["C"], r["D"], r["M"], r["N"]

    def to_owner(pd, k):
        owner = lax.rem(lon + k + 1, n)
        return C.at[pd, owner % 2, owner // 2, pl.ds(0, few)], M.at[pd, lon], (lat, owner)

    def to_next(pd, k):
        owner = lax.rem(lon + k, n)
        return D.at[pd, owner % 2, owner // 2], N.at[pd, lon], (lax.rem(lat + 1, m), owner)

    spread_here = Copies(r["ds0"], r["dr0"], to_owner)
    spread_next = Copies(r["ds1"], r["dr1"], to_next)
    Z, Q, T = r["Z"], r["Q"], r["T"]
    gather2 = Copies(
        r["as1"], r["ar1"], lambda pd, k: (Z.at[pd, zi], Z.at[pd, zi], dev(0, 2 * (k + 1)))
    )

    def partial_to(pd, k):
        peer = lax.rem(zi + k + 1, nz)
        return Q.at[pd, peer], T.at[pd, k], (lat, 2 * peer + core)

    scatter = Copies(r["rs0"], r["rr0"], partial_to)

    pl.semaphore_wait(barrier, len(greet))
    for pd in range(pds):
        for c in halo_copies:
            c.one(pd).start()
    for k in range(nz - 1):
        share_lon.one(k).start()
    for k in range(3):
        swap(k).start()
    for key in ("wo1", "we1", "wr1", "mw", "wt2", "b2", "we2", "wr2", "up"):
        loads[key].start()

    def place(index):
        return index // (WL * WW), (index // WW) % WL, index % WW

    a, b, c = place(down(WT))
    q = along(2 * WL * seg)
    r["P1"][...] = one_hot(
        (b * WD + a) * 64 + c + s1,
        ((q % (WL * seg)) // cols) * 64 + (q // (WL * seg)) * cols + q % cols,
    )
    a, b, c = place(along(WT))
    row = down(WT)
    r["U1"][...] = one_hot(row, (b * WD + a) * WW + c)

    def blocked(index):
        block, cell = index // few, index % few
        i = (cell // per_row) * 2 + block % 2
        j = (cell % hc) * 2 + block // 2
        return i * WD + (cell // hc) % WD, j

    ia, j = blocked(down(cells))
    q = along(2 * cells)
    r["B1"][...] = one_hot(
        ia * 64 + j - s1 + cols,
        ((q % cells) // cols) * 64 + jnp.where(q < cells, cols, 0) + q % cols,
    )
    q = along(cells)
    r["B0"][...] = one_hot(ia * cols + j, q)
    ia, j = blocked(along(cells))
    r["B2"][...] = one_hot(down(cells), ia * cols + j)

    def own_key(index, size, first):
        return jnp.where(
            index < size, (index // hc + first * WD) * 64 + index % hc, -1
        )

    a, b, c = place(down(WT))
    q = along(4 * fewp + 4 * hal)
    far = q >= 4 * fewp
    qh = q - 4 * fewp
    chunk = jnp.where(far, qh // hal, q // fewp)
    key = jnp.where(far, own_key(qh % hal, HALO * per_row, half), own_key(q % fewp, few, 0))
    r["P2"][...] = one_hot(
        ((b + s2) * WD + a) * 64 + c + s3, jnp.where(key < 0, -1, key + chunk * hc)
    )
    a, b, c = place(along(2 * WT) % WT)
    x = c + s3 - jnp.where(along(2 * WT) < WT, 0, cols)
    col_key = jnp.where((x >= 0) & (x < cols), ((b + s2) * WD + a) * 64 + x, -2)
    q = down(2 * fewp + 2 * hal)
    far = q >= 2 * fewp
    qh = q - 2 * fewp
    chunk = jnp.where(far, qh // hal, q // fewp)
    key = jnp.where(far, own_key(qh % hal, HALO * per_row, half), own_key(q % fewp, few, 0))
    r["U2"][...] = one_hot(jnp.where(key < 0, -1, key + chunk * hc), col_key)

    pad = jnp.zeros((fewp - few, 3 * lanes2), BF)
    for pd in range(pds):
        for z in range(nz):
            S[pd, z, few:] = pad
    for k in range(wins):
        r["K1"][k] = window_mask(rows * m - s0 - lat * rows - k * WL)
    r["K2"][...] = window_mask(half * m - s2 - lat * half)

    group = 4 if heads1 % 4 == 0 else heads1
    width = 3 * group * hd
    loads["wt"].wait()
    order = head_order(group, hd)
    for g in range(heads1 // group):
        cut = slice(g * width, (g + 1) * width)
        r["wt_o"][:, cut] = dot32(r["v_wt"][:, cut], order).astype(BF)
    loads["x0"].wait()
    loads["x1"].wait()
    for pd in range(pds):
        r["F"][pd] = dot32(r["B0"][...], flat(E[pd][0, :rows])).astype(BF)
    loads["b1"].wait()

    def fine_attention(pd):
        for cps in halo_copies:
            cps.one(pd).wait_recv()
        for k in range(wins):
            near = flat(E[pd][:, pl.ds(s0 + k * WL, WL)])
            framed = dot32(r["P1"][...], near)
            r["A"][pl.ds(k * WT, WT), :] = layer_norm(framed, r["g1"][...])
        r["tri"][...] = dot32(r["A"][...], r["wt_o"][...]).astype(BF)

        def one_group(g, carry):
            for k in range(wins):
                part = r["tri"][pl.ds(k * WT, WT), pl.ds(pl.multiple_of(g * width, 128), width)]
                total = attend(part, group, hd, lambda h: r["v_b1"][g * group + h], r["K1"][k])
                r["A"][pl.ds(k * WT, WT), pl.ds(pl.multiple_of(g * group * hd, 128), group * hd)] = (
                    total.astype(BF)
                )
            return carry

        lax.fori_loop(0, heads1 // group, one_group, 0)
        for k in range(wins):
            turned = dot32(r["U1"][...], r["A"][pl.ds(k * WT, WT), :])
            G[pd][0, pl.ds(HALO + k * WL, WL)] = turned.reshape(WL, seg, -1).astype(BF)
        for cps in back_copies:
            cps.one(pd).start()

    for pd in range(pds):
        fine_attention(pd)

    for k in range(nz - 1):
        share_lon.one(k).wait_recv()
    loads["wo2"].wait()
    for k in range(m - 1):
        share_lat.one(k).start()
    for key in ("wo1", "we1", "wr1", "mw"):
        loads[key].wait()

    def fine_tail(pd):
        for cps in back_copies:
            cps.one(pd).wait_recv()
        r["near"][...] = flat(G[pd][:, pl.ds(HALO - s0, rows)])

        def some_rows(k, carry):
            at = pl.ds(pl.multiple_of(k * (cells // 2), 16), cells // 2)
            mixed = dot32(r["B1"][at, :], r["near"][...]).astype(BF)
            attended = (r["F"][pd, at, :].astype(F32) + dot32(mixed, r["v_wo1"][...])).astype(BF)
            normed = layer_norm(attended, r["gm"][...])
            hidden = jax.nn.gelu(dot32(normed, r["v_we1"][...])).astype(BF)
            state = (attended.astype(F32) + dot32(hidden, r["v_wr1"][...])).astype(BF)
            r["state"][pd, at, :] = state.astype(F32)
            return carry

        lax.fori_loop(0, 2, some_rows, 0)
        merged = jnp.concatenate([r["state"][pd, k * few : (k + 1) * few, :] for k in range(4)], axis=1)
        coarse_in = dot32(layer_norm(merged, r["mg"][...]), r["v_mw"][...]).astype(BF)
        r["cin"][pd] = coarse_in
        X[pd, zi] = layer_norm(coarse_in, r["g2"][...])
        for k in range(nz - 1):
            gather1.one(pd, k).start()

    for pd in range(pds):
        fine_tail(pd)

    for k in range(m - 1):
        share_lat.one(k).wait_recv()
    share_core.one(0).start()
    loads["wt2"].wait()
    swap(0).wait_recv()
    order = head_order(heads2, hd)
    for k in range(2):
        r["wt2_o"][k] = dot32(r["v_wt2"][k], order).astype(BF)

    def coarse_project(pd, carry):
        for k in range(nz - 1):
            gather1.one(pd, k).wait_recv()
        given = flat(X[pd])
        theirs = dot32(given, r["wt2_o"][1 - core]).reshape(nz, few, -1).astype(BF)
        S[pd, :, pl.ds(0, few)] = theirs
        cross[0].one(pd).start()
        cross[2].one(pd).start()
        mine = dot32(given, r["wt2_o"][core]).reshape(nz, few, -1).astype(BF)
        Y[pd, core, :, pl.ds(0, few)] = mine
        for z in range(nz):
            Y[pd, core, z, few:] = pad
        cross[1].one(pd).start()
        return carry

    lax.fori_loop(0, pds, coarse_project, 0)
    loads["b2"].wait()

    def coarse_attention(pd, carry):
        for cps in cross:
            cps.one(pd).wait_recv()

        def one_window(w, carry):
            zs = [lax.rem(w + dz, nz) for dz in range(2)]
            pieces = [Y[pd, par, z] for z in zs for par in range(2)]
            pieces += [H[pd, par, z] for z in zs for par in range(2)]
            part = dot32(r["P2"][...], jnp.concatenate(pieces, axis=0))
            total = attend(part, heads2, hd, lambda h: r["v_b2"][h], r["K2"][...])
            r["V"][w] = total.astype(BF)
            return carry

        lax.fori_loop(0, nz, one_window, 0)

        def one_chip(z, carry):
            both = jnp.concatenate([r["V"][z], r["V"][lax.rem(z + nz - 1, nz)]], axis=0)
            back = dot32(r["U2"][...], both).astype(BF)
            for par in range(2):
                C[pd, par, z] = back[par * fewp : (par + 1) * fewp]
                D[pd, par, z] = back[2 * fewp + par * hal : 2 * fewp + (par + 1) * hal]
            return carry

        lax.fori_loop(0, nz, one_chip, 0)
        for k in range(n - 1):
            spread_here.one(pd, k).start()
        for k in range(n):
            spread_next.one(pd, k).start()
        M[pd, lon] = C[pd, core, zi, pl.ds(0, few)]
        return carry

    lax.fori_loop(0, pds, coarse_attention, 0)
    share_core.one(0).wait_recv()

    def coarse_output(pd, carry):
        for k in range(n - 1):
            spread_here.one(pd, k).wait_recv()
        for k in range(n):
            spread_next.one(pd, k).wait_recv()
        value = r["cin"][pd].astype(F32)
        tail = jnp.zeros((few - hal, lanes2), F32)
        for g in range(n):
            part = M[pd, g].astype(F32) + jnp.concatenate([N[pd, g].astype(F32), tail], axis=0)
            value += dot32(part.astype(BF), flat(W[g % 2, :, g // 2]))
        middle = value.astype(BF)
        r["mid"][pd] = middle
        Z[pd, zi] = layer_norm(middle, r["gm2"][...])
        for k in range(nz - 1):
            gather2.one(pd, k).start()
        return carry

    lax.fori_loop(0, pds, coarse_output, 0)
    for key in ("we2", "wr2", "up"):
        loads[key].wait()
    swap(1).wait_recv()
    swap(2).wait_recv()

    def coarse_feed(pd, carry):
        for k in range(nz - 1):
            gather2.one(pd, k).wait_recv()
        given = flat(Z[pd])
        total = None
        for k in range(2):
            hidden = jax.nn.gelu(dot32(given, r["v_we2"][k])).astype(BF)
            term = dot32(hidden, r["v_wr2"][k])
            total = term if total is None else total + term
        total = total.reshape(nz, few, -1)
        r["sum"][...] = total
        Q[pd] = total.astype(BF)
        r["own"][pd] = r["sum"][zi]
        for k in range(nz - 1):
            scatter.one(pd, k).start()
        return carry

    lax.fori_loop(0, pds, coarse_feed, 0)

    def finish(pd, carry):
        for k in range(nz - 1):
            scatter.one(pd, k).wait_recv()
        value = r["mid"][pd].astype(F32) + r["own"][pd]
        for k in range(nz - 1):
            value += T[pd, k].astype(F32)
        state = value.astype(BF)
        r["cstate"][pd] = state
        expanded = dot32(state, r["v_up"][...])
        channels = expanded.shape[1] // 4
        for k in range(4):
            at = slice(k * few, (k + 1) * few)
            cut = slice(k * channels, (k + 1) * channels)
            r["state"][pd, at, :] = r["state"][pd, at, :] + expanded[:, cut]
        r["blended"][pd] = dot32(r["B2"][...], r["state"][pd].astype(BF)).astype(BF)
        return carry

    lax.fori_loop(0, pds, finish, 0)

    for pd in range(pds):
        for cps in halo_copies + back_copies + cross:
            cps.one(pd).wait_send()
        for k in range(nz - 1):
            for cps in (gather1, gather2, scatter):
                cps.one(pd, k).wait_send()
        for k in range(n - 1):
            spread_here.one(pd, k).wait_send()
        for k in range(n):
            spread_next.one(pd, k).wait_send()
    for k in range(nz - 1):
        share_lon.one(k).wait_send()
    for k in range(m - 1):
        share_lat.one(k).wait_send()
    share_core.one(0).wait_send()
    for k in range(3):
        swap(k).wait_send()


def body(
    fine_field,
    offsets,
    fine_prenorm,
    fine_triple,
    fine_bias,
    fine_output,
    fine_midnorm,
    fine_expand,
    fine_reduce,
    merge_gain,
    merge_weight,
    coarse_prenorm,
    coarse_triple,
    coarse_bias,
    coarse_output,
    coarse_midnorm,
    coarse_expand,
    coarse_reduce,
    upsample_weight,
):
    levels, rows, cols, channels = fine_field.shape
    m = lax.axis_size("lat")
    n = lax.axis_size("lon")
    nz = n // 2
    pds = levels // WD
    wide = coarse_output.shape[1]
    heads1, heads2 = fine_bias.shape[0], coarse_bias.shape[0]
    hd = channels // heads1
    lanes2 = coarse_output.shape[0]
    assert cols == WW and rows == 2 * WL and n % 2 == 0 and nz >= 2 and pds == 2
    assert lanes2 == heads2 * hd and lanes2 % m == 0
    half, hc = rows // 2, cols // 2
    seg = WD * cols
    cells = rows * seg
    few = cells // 4
    fewp = up_to(few, 16)
    hal = up_to(HALO * WD * hc, 16)

    x = fine_field.reshape(pds, WD, rows, cols, channels).transpose(0, 2, 1, 3, 4)
    x = x.reshape(pds, rows, seg, channels)
    vmem = pl.BlockSpec(memory_space=pltpu.VMEM)
    hbm = pl.BlockSpec(memory_space=pl.ANY)
    args = [
        ("off", offsets, pl.BlockSpec(memory_space=pltpu.SMEM)),
        ("x", x, hbm),
        ("g1", fine_prenorm[None], vmem),
        ("wt", fine_triple, hbm),
        ("b1", fine_bias, hbm),
        ("wo1", fine_output, hbm),
        ("gm", fine_midnorm[None], vmem),
        ("we1", fine_expand, hbm),
        ("wr1", fine_reduce, hbm),
        ("mg", merge_gain[None], vmem),
        ("mw", merge_weight, hbm),
        ("g2", coarse_prenorm[None], vmem),
        ("wt2", coarse_triple, hbm),
        ("b2", coarse_bias, hbm),
        ("wo2", coarse_output.reshape(m, lanes2 // m, wide), hbm),
        ("gm2", coarse_midnorm[None], vmem),
        ("we2", coarse_expand, hbm),
        ("wr2", coarse_reduce, hbm),
        ("up", upsample_weight, hbm),
    ]
    outs = [
        ("blended", jax.ShapeDtypeStruct((pds, cells, channels), BF)),
        ("cstate", jax.ShapeDtypeStruct((pds, few, wide), BF)),
    ]
    sem = pltpu.SemaphoreType.DMA
    wide3 = 3 * lanes2
    scratch = [
        ("lsem", sem((14,))),
        ("v_wt", pltpu.VMEM(fine_triple.shape, BF)),
        ("wt_o", pltpu.VMEM(fine_triple.shape, BF)),
        ("v_b1", pltpu.VMEM(fine_bias.shape, F32)),
        ("v_wo1", pltpu.VMEM(fine_output.shape, BF)),
        ("v_we1", pltpu.VMEM(fine_expand.shape, BF)),
        ("v_wr1", pltpu.VMEM(fine_reduce.shape, BF)),
        ("v_mw", pltpu.VMEM(merge_weight.shape, BF)),
        ("v_wt2", pltpu.VMEM((2,) + coarse_triple.shape, BF)),
        ("wt2_o", pltpu.VMEM((2,) + coarse_triple.shape, BF)),
        ("v_b2", pltpu.VMEM(coarse_bias.shape, F32)),
        ("v_we2", pltpu.VMEM((2,) + coarse_expand.shape, BF)),
        ("v_wr2", pltpu.VMEM((2,) + coarse_reduce.shape, BF)),
        ("v_up", pltpu.VMEM(upsample_weight.shape, BF)),
        ("W", pltpu.VMEM((2, m, nz, lanes2 // m, wide), BF)),
        ("P1", pltpu.VMEM((WT, 2 * WL * seg), BF)),
        ("U1", pltpu.VMEM((WT, WT), BF)),
        ("B0", pltpu.VMEM((cells, cells), BF)),
        ("B1", pltpu.VMEM((cells, 2 * cells), BF)),
        ("B2", pltpu.VMEM((cells, cells), BF)),
        ("P2", pltpu.VMEM((WT, 4 * fewp + 4 * hal), BF)),
        ("U2", pltpu.VMEM((2 * fewp + 2 * hal, 2 * WT), BF)),
        ("K1", pltpu.VMEM((rows // WL, WT, WT), F32)),
        ("K2", pltpu.VMEM((WT, WT), F32)),
        ("F", pltpu.VMEM((pds, cells, channels), BF)),
        ("A", pltpu.VMEM((cells, channels), BF)),
        ("tri", pltpu.VMEM((cells, 3 * channels), BF)),
        ("near", pltpu.VMEM((2 * cells, channels), BF)),
        ("state", pltpu.VMEM((pds, cells, channels), F32)),
        ("cin", pltpu.VMEM((pds, few, wide), BF)),
        ("X", pltpu.VMEM((pds, nz, few, wide), BF)),
        ("Y", pltpu.VMEM((pds, 2, nz, fewp, wide3), BF)),
        ("S", pltpu.VMEM((pds, nz, fewp, wide3), BF)),
        ("H", pltpu.VMEM((pds, 2, nz, hal, wide3), BF)),
        ("V", pltpu.VMEM((nz, WT, lanes2), BF)),
        ("C", pltpu.VMEM((pds, 2, nz, fewp, lanes2), BF)),
        ("D", pltpu.VMEM((pds, 2, nz, hal, lanes2), BF)),
        ("M", pltpu.VMEM((pds, n, few, lanes2), BF)),
        ("N", pltpu.VMEM((pds, n, hal, lanes2), BF)),
        ("mid", pltpu.VMEM((pds, few, wide), BF)),
        ("Z", pltpu.VMEM((pds, nz, few, wide), BF)),
        ("sum", pltpu.VMEM((nz, few, wide), F32)),
        ("own", pltpu.VMEM((pds, few, wide), F32)),
        ("Q", pltpu.VMEM((pds, nz, few, wide), BF)),
        ("T", pltpu.VMEM((pds, nz - 1, few, wide), BF)),
    ]
    for pd in range(pds):
        for name in ("E", "G"):
            scratch.append((name + str(pd), pltpu.VMEM((2, rows + HALO, seg, channels), BF)))
    for name in ("h", "b", "c"):
        for k in range(3):
            scratch += [("%ss%d" % (name, k), sem((pds,))), ("%sr%d" % (name, k), sem((pds,)))]
    for s, d, shape in (
        ("ws0", "wr0", (nz - 1,)),
        ("ws1", "wr1s", (m - 1,)),
        ("ws2", "wr2s", (1,)),
        ("ss", "sr", (3,)),
        ("as0", "ar0", (pds, nz - 1)),
        ("as1", "ar1", (pds, nz - 1)),
        ("ds0", "dr0", (pds, n - 1)),
        ("ds1", "dr1", (pds, n)),
        ("rs0", "rr0", (pds, nz - 1)),
    ):
        scratch += [(s, sem(shape)), (d, sem(shape))]

    cfg = dict(m=m, n=n, pds=pds, rows=rows, cols=cols, heads1=heads1, heads2=heads2, hd=hd)
    names = [a[0] for a in args] + [o[0] for o in outs] + [s[0] for s in scratch]
    blended, state = pl.pallas_call(
        functools.partial(step_kernel, cfg, names),
        out_shape=[o[1] for o in outs],
        in_specs=[a[2] for a in args],
        out_specs=[vmem, vmem],
        scratch_shapes=[s[1] for s in scratch],
        compiler_params=pltpu.CompilerParams(
            collective_id=0, has_side_effects=True, vmem_limit_bytes=63 << 20
        ),
    )(*[a[1] for a in args])
    blended = blended.reshape(pds, rows, WD, cols, channels).transpose(0, 2, 1, 3, 4)
    state = state.reshape(pds, half, WD, hc, wide).transpose(0, 2, 1, 3, 4)
    return (
        blended.reshape(levels, rows, cols, channels),
        state.reshape(levels, half, hc, wide),
    )


def solution(mesh):
    placed = (
        P(None, "lat", "lon", None),
        P(),
        P(),
        P(),
        P(),
        P(),
        P(),
        P(),
        P(),
        P(),
        P(),
        P(),
        P(None, "lon"),
        P("lon", None, None),
        P("lon", None),
        P(),
        P(None, "lon"),
        P("lon", None),
        P(),
    )
    return jax.shard_map(
        body,
        mesh=mesh,
        in_specs=placed,
        out_specs=(P(None, "lat", "lon", None), P(None, "lat", "lon", None)),
        check_vma=False,
    )
```

time: 245 us -> 144 us (0.59)
  waiting for transfers between devices: 134 us -> 0 us
  Pallas kernels: 34.7 us -> 134 us
  matrix products: 16.3 us -> 0 us
  starting transfers between devices: 15.9 us -> 0 us
  between operations: 15.5 us -> 0.68 us
  blocking collectives: 13.2 us -> 0 us
  other arithmetic: 5.49 us -> 0 us
    pallas_call x6 -> x1, Pallas kernels: 34.7 us -> 134 us  [body(): pl.pallas_call(functools.partial(step_kernel, cfg, names), out_shape=[o[1...]
    all_gather x3 -> x0, waiting for transfers between devices: 60.2 us -> none  [the longest x1 30.4 us: body(): band_cells = lax.all_gather(coarse_in, 'lon', axis=0, tiled=True)]
    ppermute x8 -> x0, waiting for transfers between devices: 37 us -> none  [the longest x6 30.9 us: moved(): return lax.ppermute(block, axes[0], pairs)]
    reduce_scatter x1 -> x0, waiting for transfers between devices: 36.4 us -> none  [body(): lax.psum_scatter(product, 'lon', scatter_dimension=0, tiled=True)]
    dot_general x10 -> x0, matrix products: 16.3 us -> none  [dot32(): return jnp.dot(left, right, preferred_element_type=F32)]
    ppermute x8 -> x0, starting transfers between devices: 15.5 us -> none  [the longest x6 14.4 us: moved(): return lax.ppermute(block, axes[0], pairs)]
    all_to_all x1 -> x0, blocking collectives: 13.2 us -> none  [body(): lax.all_to_all(mixed2.reshape(group_count, few, mixed_width), 'lon', spli...]
    unnamed x50 -> x2, local copies, waits for them, and re-layouts: 8.81 us -> 0.01 us
  transfers between devices with their start and end apart: 12 -> 0, of which waited for: 8 -> 0; matrix products, arithmetic and copies ran while one was open for 5% -> 0% of each run, Pallas kernels for 3% -> 0%
where the time goes in v1:
time: 144 us; the launch traced here: 143 us
  Pallas kernels  134 us (93%)
  local copies, waits for them, and re-layouts  7.97 us (6%)
    pallas_call x1, Pallas kernels, body(): pl.pallas_call(functools.partial(step_kernel, cfg, names), out_shape=[o[1...  134 us

profile of v1, /device:TPU:0, one launch (start us, length us, event | category | flops | bytes accessed | tf_op | source)
XLA Modules:
  0.0 142.6 jit_solution(13550692089174456919)
XLA Ops:
  0.6 1.9 %reshape.25 = bf16[2,2,12,12,512]{4,1,0,3,2:T(2,128)(2,1)S(1)} reshape(bf16[4,12,12,512]{3,0,2,1:T(4,128)(2,1)} %param.19) | data formatting | bytes 1179648 | tf_op jit(solution)/shard_map/reshape | solution.py:566
  2.5 0.5 copy.28
  3.1 0.9 copy.29.refs_1_
  3.9 134.0 %shard_map.194 = (bf16[2,288,512]{2,1,0:T(8,128)(2,1)}, bf16[2,72,1024]{2,1,0:T(8,128)(2,1)}) custom-call(s32[4]{0:T(128)} %refs_0_.1, bf16[2,12,24,512]{3,2,1,0:T(8,128)(2,1)} %copy.29.refs_1_, f32[1,512]{1,0:T(1,128)} %bitcast.28, bf16[512,1536]{1,0:T(8,128)(2,1)} %refs_3_.1, f32[16,144,144]{2,1,0:T(8,128)} %refs_4_.1, bf16[512,512]{1,0:T(8,128)(2,1)} %refs_5_.1, ...), custom_call_target="tpu_custom_call" | custom-call | tf_op jit(solution)/shard_map/pallas_call | solution.py:665
  137.9 0.0 copy-start
  137.9 1.7 %copy.30 = bf16[2,288,512]{2,0,1:T(2,128)(2,1)S(1)} copy(bf16[2,288,512]{2,1,0:T(8,128)(2,1)} %get-tuple-element.4) | data formatting | bytes 1179648 | tf_op jit(solution)/shard_map/pallas_call | solution.py:665
  139.6 0.5 copy.31
  140.2 1.0 reshape.29
  141.2 0.0 copy-done
  141.2 0.3 copy.32
  141.5 0.2 copy.33
  141.8 0.8 reshape.31
Async XLA Ops:
  137.9 3.3 %copy-start = (bf16[2,72,1024]{2,1,0:T(8,128)(2,1)S(1)}, bf16[2,72,1024]{2,1,0:T(8,128)(2,1)}, u32[]{:S(2)}) copy-start(bf16[2,72,1024]{2,1,0:T(8,128)(2,1)} %get-tuple-element.5) | copy-start | bytes 884740

commit v2 on v1

--- a/solution.py
+++ b/solution.py
@@ -182,7 +182,7 @@
     ]
     W = r["W"]
     share_lon = Copies(
-        r["ws0"], r["wr0"], lambda k: (r["wo2"].at[lat], W.at[core, lat, zi], dev(0, 2 * (k + 1)))
+        r["ws0"], r["wr0"], lambda k: (W.at[core, lat, zi], W.at[core, lat, zi], dev(0, 2 * (k + 1)))
     )
     share_lat = Copies(r["ws1"], r["wr1s"], lambda k: (W.at[core, lat], W.at[core, lat], dev(k + 1, 0)))
     share_core = Copies(r["ws2"], r["wr2s"], lambda k: (W.at[core], W.at[core], (lat, buddy)))
@@ -199,16 +199,69 @@
         )
 
     X, Y, S, H = r["X"], r["Y"], r["S"], r["H"]
-    gather1 = Copies(
-        r["as0"], r["ar0"], lambda pd, k: (X.at[pd, zi], X.at[pd, zi], dev(0, 2 * (k + 1)))
-    )
+
+    def relay(buf, sends, recvs):
+        def hop(pd, z, way, reach):
+            step = 2 - 4 * way
+            return pltpu.make_async_remote_copy(
+                buf.at[pd, z],
+                buf.at[pd, z],
+                r[sends].at[pd, way, reach - 1],
+                r[recvs].at[pd, way, reach - 1],
+                device_id=(lat, lon + step),
+                device_id_type=MESH,
+            )
+
+        def pass_on(pd, z, way, reach, act):
+            @pl.when(jnp.where(way == 0, zi < nz - 1, zi > 0))
+            def _():
+                act(hop(pd, z, way, reach))
+
+        def start(pd):
+            for way in range(2):
+                pass_on(pd, zi, way, 1, lambda c: c.start())
+
+        def turn(j):
+            both = jnp.minimum(zi, nz - 1 - zi)
+            even = j < 2 * both
+            way = jnp.where(even, j % 2, jnp.where(zi > nz - 1 - zi, 0, 1))
+            reach = jnp.where(even, j // 2 + 1, j - both + 1)
+            return zi - reach * (1 - 2 * way), way, reach
+
+        def arrive(pd, j):
+            z, way, reach = turn(j)
+            hop(pd, z, way, reach).wait_recv()
+
+            @pl.when(reach < nz - 1)
+            def _():
+                pass_on(pd, z, way, reach + 1, lambda c: c.start())
+
+            return z
+
+        def drain(pd):
+            def one(j, carry):
+                z, way, reach = turn(j)
+
+                @pl.when(reach < nz - 1)
+                def _():
+                    pass_on(pd, z, way, reach + 1, lambda c: c.wait_send())
+
+                return carry
+
+            for way in range(2):
+                pass_on(pd, zi, way, 1, lambda c: c.wait_send())
+            lax.fori_loop(0, nz - 1, one, 0)
+
+        return start, arrive, drain
+
+    gather1_start, gather1_arrive, gather1_drain = relay(X, "as0", "ar0")
     cross = [
         Copies(r["cs%d" % k], r["cr%d" % k], make)
         for k, make in enumerate(
             (
-                lambda pd: (S.at[pd], Y.at[pd, core], (lat, buddy)),
-                lambda pd: (Y.at[pd, core, :, pl.ds(0, hal)], H.at[pd, core], dev(-1, 0)),
-                lambda pd: (S.at[pd, :, pl.ds(0, hal)], H.at[pd, core], (lax.rem(lat + m - 1, m), buddy)),
+                lambda pd, z: (S.at[pd, z], Y.at[pd, core, z], (lat, buddy)),
+                lambda pd, z: (Y.at[pd, core, z, pl.ds(0, hal)], H.at[pd, core, z], dev(-1, 0)),
+                lambda pd, z: (S.at[pd, z, pl.ds(0, hal)], H.at[pd, core, z], (lax.rem(lat + m - 1, m), buddy)),
             )
         )
     ]
@@ -225,26 +278,28 @@
     spread_here = Copies(r["ds0"], r["dr0"], to_owner)
     spread_next = Copies(r["ds1"], r["dr1"], to_next)
     Z, Q, T = r["Z"], r["Q"], r["T"]
-    gather2 = Copies(
-        r["as1"], r["ar1"], lambda pd, k: (Z.at[pd, zi], Z.at[pd, zi], dev(0, 2 * (k + 1)))
-    )
-
-    def partial_to(pd, k):
-        peer = lax.rem(zi + k + 1, nz)
-        return Q.at[pd, peer], T.at[pd, k], (lat, 2 * peer + core)
-
-    scatter = Copies(r["rs0"], r["rr0"], partial_to)
-
-    pl.semaphore_wait(barrier, len(greet))
-    for pd in range(pds):
-        for c in halo_copies:
-            c.one(pd).start()
-    for k in range(nz - 1):
-        share_lon.one(k).start()
-    for k in range(3):
-        swap(k).start()
-    for key in ("wo1", "we1", "wr1", "mw", "wt2", "b2", "we2", "wr2", "up"):
-        loads[key].start()
+    gather2_start, gather2_arrive, gather2_drain = relay(Z, "as1", "ar1")
+
+    def partial_to(pd, z):
+        return pltpu.make_async_remote_copy(
+            Q.at[pd, z],
+            T.at[pd, zi],
+            r["rs0"].at[pd, z],
+            r["rr0"].at[pd, zi],
+            device_id=(lat, 2 * z + core),
+            device_id_type=MESH,
+        )
+
+    def partial_from(pd, z):
+        return pltpu.make_async_remote_copy(
+            Q.at[pd, z],
+            T.at[pd, z],
+            r["rs0"].at[pd, z],
+            r["rr0"].at[pd, z],
+            device_id=(lat, 2 * z + core),
+            device_id_type=MESH,
+        )
+
 
     def place(index):
         return index // (WL * WW), (index // WW) % WL, index % WW
@@ -308,6 +363,18 @@
         r["K1"][k] = window_mask(rows * m - s0 - lat * rows - k * WL)
     r["K2"][...] = window_mask(half * m - s2 - lat * half)
 
+    pl.semaphore_wait(barrier, len(greet))
+    for pd in range(pds):
+        for cps in halo_copies:
+            cps.one(pd).start()
+    loads["wo2"].wait()
+    for k in range(nz - 1):
+        share_lon.one(k).start()
+    for k in range(3):
+        swap(k).start()
+    for key in ("we2", "wr2", "wt2", "wo1", "we1", "wr1", "mw", "b2", "up"):
+        loads[key].start()
+
     group = 4 if heads1 % 4 == 0 else heads1
     width = 3 * group * hd
     loads["wt"].wait()
@@ -351,9 +418,13 @@
 
     for k in range(nz - 1):
         share_lon.one(k).wait_recv()
-    loads["wo2"].wait()
     for k in range(m - 1):
         share_lat.one(k).start()
+    loads["wt2"].wait()
+    swap(0).wait_recv()
+    order = head_order(heads2, hd)
+    for k in range(2):
+        r["wt2_o"][k] = dot32(r["v_wt2"][k], order).astype(BF)
     for key in ("wo1", "we1", "wr1", "mw"):
         loads[key].wait()
 
@@ -377,42 +448,42 @@
         coarse_in = dot32(layer_norm(merged, r["mg"][...]), r["v_mw"][...]).astype(BF)
         r["cin"][pd] = coarse_in
         X[pd, zi] = layer_norm(coarse_in, r["g2"][...])
-        for k in range(nz - 1):
-            gather1.one(pd, k).start()
+        gather1_start(pd)
 
     for pd in range(pds):
         fine_tail(pd)
 
+    for pd in range(pds):
+        for z in range(nz):
+            Y[pd, core, z, few:] = pad
+
+    def coarse_project(pd):
+        def project(z):
+            given = X[pd, z]
+            S[pd, z, pl.ds(0, few)] = dot32(given, r["wt2_o"][1 - core]).astype(BF)
+            cross[0].one(pd, z).start()
+            cross[2].one(pd, z).start()
+            Y[pd, core, z, pl.ds(0, few)] = dot32(given, r["wt2_o"][core]).astype(BF)
+            cross[1].one(pd, z).start()
+
+        def one_chunk(j, carry):
+            project(gather1_arrive(pd, j))
+            return carry
+
+        project(zi)
+        lax.fori_loop(0, nz - 1, one_chunk, 0)
+
+    for pd in range(pds):
+        coarse_project(pd)
     for k in range(m - 1):
         share_lat.one(k).wait_recv()
     share_core.one(0).start()
-    loads["wt2"].wait()
-    swap(0).wait_recv()
-    order = head_order(heads2, hd)
-    for k in range(2):
-        r["wt2_o"][k] = dot32(r["v_wt2"][k], order).astype(BF)
-
-    def coarse_project(pd, carry):
-        for k in range(nz - 1):
-            gather1.one(pd, k).wait_recv()
-        given = flat(X[pd])
-        theirs = dot32(given, r["wt2_o"][1 - core]).reshape(nz, few, -1).astype(BF)
-        S[pd, :, pl.ds(0, few)] = theirs
-        cross[0].one(pd).start()
-        cross[2].one(pd).start()
-        mine = dot32(given, r["wt2_o"][core]).reshape(nz, few, -1).astype(BF)
-        Y[pd, core, :, pl.ds(0, few)] = mine
+    loads["b2"].wait()
+
+    def coarse_attention(pd, carry):
         for z in range(nz):
-            Y[pd, core, z, few:] = pad
-        cross[1].one(pd).start()
-        return carry
-
-    lax.fori_loop(0, pds, coarse_project, 0)
-    loads["b2"].wait()
-
-    def coarse_attention(pd, carry):
-        for cps in cross:
-            cps.one(pd).wait_recv()
+            for cps in cross:
+                cps.one(pd, z).wait_recv()
 
         def one_window(w, carry):
             zs = [lax.rem(w + dz, nz) for dz in range(2)]
@@ -441,7 +512,8 @@
         M[pd, lon] = C[pd, core, zi, pl.ds(0, few)]
         return carry
 
-    lax.fori_loop(0, pds, coarse_attention, 0)
+    coarse_attention(0, 0)
+    coarse_attention(1, 0)
     share_core.one(0).wait_recv()
 
     def coarse_output(pd, carry):
@@ -453,45 +525,50 @@
         tail = jnp.zeros((few - hal, lanes2), F32)
         for g in range(n):
             part = M[pd, g].astype(F32) + jnp.concatenate([N[pd, g].astype(F32), tail], axis=0)
-            value += dot32(part.astype(BF), flat(W[g % 2, :, g // 2]))
+            rows_g = W[g % 2, :, g // 2]
+            rows_g = rows_g.reshape(lanes2, -1) if rows_g.shape[1] % 16 == 0 else flat(rows_g)
+            value += dot32(part.astype(BF), rows_g)
         middle = value.astype(BF)
         r["mid"][pd] = middle
         Z[pd, zi] = layer_norm(middle, r["gm2"][...])
-        for k in range(nz - 1):
-            gather2.one(pd, k).start()
+        gather2_start(pd)
         return carry
 
-    lax.fori_loop(0, pds, coarse_output, 0)
+    coarse_output(0, 0)
+    coarse_output(1, 0)
     for key in ("we2", "wr2", "up"):
         loads[key].wait()
     swap(1).wait_recv()
     swap(2).wait_recv()
 
-    def coarse_feed(pd, carry):
-        for k in range(nz - 1):
-            gather2.one(pd, k).wait_recv()
-        given = flat(Z[pd])
-        total = None
-        for k in range(2):
-            hidden = jax.nn.gelu(dot32(given, r["v_we2"][k])).astype(BF)
-            term = dot32(hidden, r["v_wr2"][k])
-            total = term if total is None else total + term
-        total = total.reshape(nz, few, -1)
-        r["sum"][...] = total
-        Q[pd] = total.astype(BF)
-        r["own"][pd] = r["sum"][zi]
-        for k in range(nz - 1):
-            scatter.one(pd, k).start()
-        return carry
-
-    lax.fori_loop(0, pds, coarse_feed, 0)
+    def coarse_feed(pd):
+        def feed(z):
+            given = Z[pd, z]
+            total = None
+            for k in range(2):
+                hidden = jax.nn.gelu(dot32(given, r["v_we2"][k])).astype(BF)
+                term = dot32(hidden, r["v_wr2"][k])
+                total = term if total is None else total + term
+            return total
+
+        def one_chunk(j, carry):
+            z = gather2_arrive(pd, j)
+            Q[pd, z] = feed(z).astype(BF)
+            partial_to(pd, z).start()
+            return carry
+
+        r["own"][pd] = feed(zi)
+        lax.fori_loop(0, nz - 1, one_chunk, 0)
+
+    for pd in range(pds):
+        coarse_feed(pd)
 
     def finish(pd, carry):
-        for k in range(nz - 1):
-            scatter.one(pd, k).wait_recv()
         value = r["mid"][pd].astype(F32) + r["own"][pd]
-        for k in range(nz - 1):
-            value += T[pd, k].astype(F32)
+        for k in range(1, nz):
+            z = lax.rem(zi + k, nz)
+            partial_from(pd, z).wait_recv()
+            value += T[pd, z].astype(F32)
         state = value.astype(BF)
         r["cstate"][pd] = state
         expanded = dot32(state, r["v_up"][...])
@@ -506,11 +583,15 @@
     lax.fori_loop(0, pds, finish, 0)
 
     for pd in range(pds):
-        for cps in halo_copies + back_copies + cross:
+        for cps in halo_copies + back_copies:
             cps.one(pd).wait_send()
-        for k in range(nz - 1):
-            for cps in (gather1, gather2, scatter):
-                cps.one(pd, k).wait_send()
+        for z in range(nz):
+            for cps in cross:
+                cps.one(pd, z).wait_send()
+        gather1_drain(pd)
+        gather2_drain(pd)
+        for k in range(1, nz):
+            partial_to(pd, lax.rem(zi + k, nz)).wait_send()
         for k in range(n - 1):
             spread_here.one(pd, k).wait_send()
         for k in range(n):
@@ -636,27 +717,26 @@
         ("N", pltpu.VMEM((pds, n, hal, lanes2), BF)),
         ("mid", pltpu.VMEM((pds, few, wide), BF)),
         ("Z", pltpu.VMEM((pds, nz, few, wide), BF)),
-        ("sum", pltpu.VMEM((nz, few, wide), F32)),
         ("own", pltpu.VMEM((pds, few, wide), F32)),
         ("Q", pltpu.VMEM((pds, nz, few, wide), BF)),
-        ("T", pltpu.VMEM((pds, nz - 1, few, wide), BF)),
+        ("T", pltpu.VMEM((pds, nz, few, wide), BF)),
     ]
     for pd in range(pds):
         for name in ("E", "G"):
             scratch.append((name + str(pd), pltpu.VMEM((2, rows + HALO, seg, channels), BF)))
-    for name in ("h", "b", "c"):
+    for name, shape in (("h", (pds,)), ("b", (pds,)), ("c", (pds, nz))):
         for k in range(3):
-            scratch += [("%ss%d" % (name, k), sem((pds,))), ("%sr%d" % (name, k), sem((pds,)))]
+            scratch += [("%ss%d" % (name, k), sem(shape)), ("%sr%d" % (name, k), sem(shape))]
     for s, d, shape in (
         ("ws0", "wr0", (nz - 1,)),
         ("ws1", "wr1s", (m - 1,)),
         ("ws2", "wr2s", (1,)),
         ("ss", "sr", (3,)),
-        ("as0", "ar0", (pds, nz - 1)),
-        ("as1", "ar1", (pds, nz - 1)),
+        ("as0", "ar0", (pds, 2, nz - 1)),
+        ("as1", "ar1", (pds, 2, nz - 1)),
         ("ds0", "dr0", (pds, n - 1)),
         ("ds1", "dr1", (pds, n)),
-        ("rs0", "rr0", (pds, nz - 1)),
+        ("rs0", "rr0", (pds, nz)),
     ):
         scratch += [(s, sem(shape)), (d, sem(shape))]
 

time: 144 us -> 134 us (0.931)
  Pallas kernels: 134 us -> 125 us
    pallas_call x1, Pallas kernels: 134 us -> 125 us  [body(): pl.pallas_call(functools.partial(step_kernel, cfg, names), out_shape=[o[1...]
where the time goes in v2:
time: 134 us; the launch traced here: 133 us
  Pallas kernels  125 us (93%)
  local copies, waits for them, and re-layouts  7.97 us (6%)
    pallas_call x1, Pallas kernels, body(): pl.pallas_call(functools.partial(step_kernel, cfg, names), out_shape=[o[1...  125 us

profile of v2, /device:TPU:0, one launch (start us, length us, event | category | flops | bytes accessed | tf_op | source)
XLA Modules:
  0.0 133.5 jit_solution(7871056886356860877)
XLA Ops:
  0.6 1.9 %reshape.25 = bf16[2,2,12,12,512]{4,1,0,3,2:T(2,128)(2,1)S(1)} reshape(bf16[4,12,12,512]{3,0,2,1:T(4,128)(2,1)} %param.19) | data formatting | bytes 1179648 | tf_op jit(solution)/shard_map/reshape | solution.py:647
  2.5 0.5 copy.28
  3.1 0.9 copy.29.refs_1_
  3.9 124.8 %shard_map.194 = (bf16[2,288,512]{2,1,0:T(8,128)(2,1)}, bf16[2,72,1024]{2,1,0:T(8,128)(2,1)}) custom-call(s32[4]{0:T(128)} %refs_0_.1, bf16[2,12,24,512]{3,2,1,0:T(8,128)(2,1)} %copy.29.refs_1_, f32[1,512]{1,0:T(1,128)} %bitcast.28, bf16[512,1536]{1,0:T(8,128)(2,1)} %refs_3_.1, f32[16,144,144]{2,1,0:T(8,128)} %refs_4_.1, bf16[512,512]{1,0:T(8,128)(2,1)} %refs_5_.1, ...), custom_call_target="tpu_custom_call" | custom-call | tf_op jit(solution)/shard_map/pallas_call | solution.py:745
  128.8 0.0 copy-start
  128.8 1.7 %copy.30 = bf16[2,288,512]{2,0,1:T(2,128)(2,1)S(1)} copy(bf16[2,288,512]{2,1,0:T(8,128)(2,1)} %get-tuple-element.4) | data formatting | bytes 1179648 | tf_op jit(solution)/shard_map/pallas_call | solution.py:745
  130.5 0.5 copy.31
  131.0 1.0 reshape.29
  132.1 0.0 copy-done
  132.1 0.3 copy.32
  132.4 0.2 copy.33
  132.6 0.8 reshape.31
Async XLA Ops:
  128.8 3.3 %copy-start = (bf16[2,72,1024]{2,1,0:T(8,128)(2,1)S(1)}, bf16[2,72,1024]{2,1,0:T(8,128)(2,1)}, u32[]{:S(2)}) copy-start(bf16[2,72,1024]{2,1,0:T(8,128)(2,1)} %get-tuple-element.5) | copy-start | bytes 884740

commit v3 on v2

--- a/solution.py
+++ b/solution.py
@@ -103,6 +103,32 @@
         )
 
 
+def blocked(index, cells, few, per_row, hc):
+    block, cell = index // few, index % few
+    i = (cell // per_row) * 2 + block % 2
+    j = (cell % hc) * 2 + block // 2
+    return i * WD + (cell // hc) % WD, j
+
+
+def arrange_kernel(fine_ref, coarse_ref, fine_out, coarse_out):
+    pds, cells, _ = fine_ref.shape
+    few = coarse_ref.shape[1]
+    _, cols, levels, _ = fine_out.shape
+    hc = cols // 2
+    per_row = WD * hc
+    q = along(pds * cells)
+    ia, j = blocked(q % cells, cells, few, per_row, hc)
+    chosen = one_hot(down(pds * cells), ((ia // WD) * cols + j) * levels + (q // cells) * WD + ia % WD)
+    fine_out[...] = dot32(chosen, flat(fine_ref[...])).reshape(fine_out.shape).astype(BF)
+    q = along(pds * few)
+    cell = q % few
+    chosen = one_hot(
+        down(pds * few),
+        ((cell // per_row) * hc + cell % hc) * levels + (q // few) * WD + (cell // hc) % WD,
+    )
+    coarse_out[...] = dot32(chosen, flat(coarse_ref[...])).reshape(coarse_out.shape).astype(BF)
+
+
 def step_kernel(cfg, names, *refs):
     r = dict(zip(names, refs))
     m, n, nz = cfg["m"], cfg["n"], cfg["n"] // 2
@@ -141,8 +167,7 @@
     E = [r["E%d" % pd] for pd in range(pds)]
     G = [r["G%d" % pd] for pd in range(pds)]
     loads = {
-        "x0": local(0, r["x"].at[0], E[0].at[0, pl.ds(0, rows)]),
-        "x1": local(1, r["x"].at[1], E[1].at[0, pl.ds(0, rows)]),
+        "x": local(0, r["x"], r["v_x"]),
         "wt": local(2, r["wt"], r["v_wt"]),
         "b1": local(3, r["b1"], r["v_b1"]),
         "wo1": local(4, r["wo1"], r["v_wo1"]),
@@ -156,16 +181,16 @@
         "up": local(12, r["up"], r["v_up"]),
         "wo2": local(13, r["wo2"].at[lat], r["W"].at[core, lat, zi]),
     }
-    for key in ("x0", "x1", "wt", "b1", "wo2"):
+    for key in ("x", "wt", "b1", "wo2"):
         loads[key].start()
 
     halo_copies = [
         Copies(r["hs%d" % k], r["hr%d" % k], make)
         for k, make in enumerate(
             (
-                lambda pd: (r["x"].at[pd], E[pd].at[1, pl.ds(0, rows)], dev(0, -1)),
-                lambda pd: (r["x"].at[pd, pl.ds(0, HALO)], E[pd].at[0, pl.ds(rows, HALO)], dev(-1, 0)),
-                lambda pd: (r["x"].at[pd, pl.ds(0, HALO)], E[pd].at[1, pl.ds(rows, HALO)], dev(-1, -1)),
+                lambda pd: (E[pd].at[0, pl.ds(0, rows)], E[pd].at[1, pl.ds(0, rows)], dev(0, -1)),
+                lambda pd: (E[pd].at[0, pl.ds(0, HALO)], E[pd].at[0, pl.ds(rows, HALO)], dev(-1, 0)),
+                lambda pd: (E[pd].at[0, pl.ds(0, HALO)], E[pd].at[1, pl.ds(rows, HALO)], dev(-1, -1)),
             )
         )
     ]
@@ -277,29 +302,87 @@
 
     spread_here = Copies(r["ds0"], r["dr0"], to_owner)
     spread_next = Copies(r["ds1"], r["dr1"], to_next)
-    Z, Q, T = r["Z"], r["Q"], r["T"]
+    Z, Q, T, R = r["Z"], r["Q"], r["T"], r["R"]
     gather2_start, gather2_arrive, gather2_drain = relay(Z, "as1", "ar1")
 
-    def partial_to(pd, z):
-        return pltpu.make_async_remote_copy(
-            Q.at[pd, z],
-            T.at[pd, zi],
-            r["rs0"].at[pd, z],
-            r["rr0"].at[pd, zi],
-            device_id=(lat, 2 * z + core),
-            device_id_type=MESH,
+    def partial(pd, z):
+        way = jnp.where(z > zi, 0, 1)
+        step = 2 - 4 * way
+
+        def message(dst, recv, target):
+            return pltpu.make_async_remote_copy(
+                Q.at[pd, z], dst, r["rs0"].at[pd, z], recv, device_id=(lat, target), device_id_type=MESH
+            )
+
+        final = message(T.at[pd, way], r["rr0"].at[pd, way], lon + step)
+        between = message(R.at[pd, z], r["rr1"].at[pd, z], lon + step)
+        direct = message(T.at[pd, 2], r["rr0"].at[pd, 2], 2 * z + core)
+        return jnp.abs(z - zi), final, between, direct
+
+    def partial_start(pd, z):
+        reach, final, between, direct = partial(pd, z)
+
+        @pl.when(reach == 1)
+        def _():
+            final.start()
+
+        straight = nz > 2 and pd == pds - 1
+
+        @pl.when((reach > 1) & (reach < (nz - 1 if straight else nz)))
+        def _():
+            between.start()
+
+        if straight:
+
+            @pl.when(reach == nz - 1)
+            def _():
+                direct.start()
+
+    def adds(pd, z):
+        first = ((z == 0) & (zi == nz - 2)) | ((z == nz - 1) & (zi == 1))
+        inner = (zi > 0) & (zi < nz - 1)
+        return inner & jnp.logical_not(first) if pd == pds - 1 else inner
+
+    def partial_pass(pd, j):
+        above, below = nz - 1 - zi, zi
+        up = jnp.where(2 * zi < nz, j < above, j >= below)
+        z = jnp.where(
+            2 * zi < nz,
+            jnp.where(up, zi + 1 + j, zi - 1 - (j - above)),
+            jnp.where(up, zi + 1 + (j - below), zi - 1 - j),
         )
 
-    def partial_from(pd, z):
-        return pltpu.make_async_remote_copy(
-            Q.at[pd, z],
-            T.at[pd, z],
-            r["rs0"].at[pd, z],
-            r["rr0"].at[pd, z],
-            device_id=(lat, 2 * z + core),
-            device_id_type=MESH,
-        )
-
+        @pl.when(adds(pd, z))
+        def _():
+            partial(pd, z)[2].wait_recv()
+            Q[pd, z] = (r["part"][pd, z] + R[pd, z].astype(F32)).astype(BF)
+            partial_start(pd, z)
+
+    piece = WL * seg
+    q = down(pds * piece)
+    inside = q % piece
+    to_pairs = one_hot(
+        ((inside // seg) * cols + inside % cols) * (pds * WD) + (q // piece) * WD + (inside % seg) // cols,
+        along(pds * piece),
+    )
+    loads["x"].wait()
+    for k in range(wins):
+        turned = dot32(to_pairs, flat(r["v_x"][k * WL : (k + 1) * WL]))
+        for pd in range(pds):
+            E[pd][0, k * WL : (k + 1) * WL] = (
+                turned[pd * piece : (pd + 1) * piece].reshape(WL, seg, -1).astype(BF)
+            )
+    pl.semaphore_wait(barrier, len(greet))
+    for pd in range(pds):
+        for cps in halo_copies:
+            cps.one(pd).start()
+    loads["wo2"].wait()
+    for k in range(nz - 1):
+        share_lon.one(k).start()
+    for k in range(3):
+        swap(k).start()
+    for key in ("we2", "wr2", "wt2", "wo1", "we1", "wr1", "mw", "b2", "up"):
+        loads[key].start()
 
     def place(index):
         return index // (WL * WW), (index // WW) % WL, index % WW
@@ -314,13 +397,7 @@
     row = down(WT)
     r["U1"][...] = one_hot(row, (b * WD + a) * WW + c)
 
-    def blocked(index):
-        block, cell = index // few, index % few
-        i = (cell // per_row) * 2 + block % 2
-        j = (cell % hc) * 2 + block // 2
-        return i * WD + (cell // hc) % WD, j
-
-    ia, j = blocked(down(cells))
+    ia, j = blocked(down(cells), cells, few, per_row, hc)
     q = along(2 * cells)
     r["B1"][...] = one_hot(
         ia * 64 + j - s1 + cols,
@@ -328,9 +405,6 @@
     )
     q = along(cells)
     r["B0"][...] = one_hot(ia * cols + j, q)
-    ia, j = blocked(along(cells))
-    r["B2"][...] = one_hot(down(cells), ia * cols + j)
-
     def own_key(index, size, first):
         return jnp.where(
             index < size, (index // hc + first * WD) * 64 + index % hc, -1
@@ -363,18 +437,6 @@
         r["K1"][k] = window_mask(rows * m - s0 - lat * rows - k * WL)
     r["K2"][...] = window_mask(half * m - s2 - lat * half)
 
-    pl.semaphore_wait(barrier, len(greet))
-    for pd in range(pds):
-        for cps in halo_copies:
-            cps.one(pd).start()
-    loads["wo2"].wait()
-    for k in range(nz - 1):
-        share_lon.one(k).start()
-    for k in range(3):
-        swap(k).start()
-    for key in ("we2", "wr2", "wt2", "wo1", "we1", "wr1", "mw", "b2", "up"):
-        loads[key].start()
-
     group = 4 if heads1 % 4 == 0 else heads1
     width = 3 * group * hd
     loads["wt"].wait()
@@ -382,8 +444,6 @@
     for g in range(heads1 // group):
         cut = slice(g * width, (g + 1) * width)
         r["wt_o"][:, cut] = dot32(r["v_wt"][:, cut], order).astype(BF)
-    loads["x0"].wait()
-    loads["x1"].wait()
     for pd in range(pds):
         r["F"][pd] = dot32(r["B0"][...], flat(E[pd][0, :rows])).astype(BF)
     loads["b1"].wait()
@@ -553,8 +613,19 @@
 
         def one_chunk(j, carry):
             z = gather2_arrive(pd, j)
-            Q[pd, z] = feed(z).astype(BF)
-            partial_to(pd, z).start()
+            term = feed(z)
+
+            @pl.when(adds(pd, z))
+            def _():
+                r["part"][pd, z] = term
+
+            @pl.when(jnp.logical_not(adds(pd, z)))
+            def _():
+                Q[pd, z] = term.astype(BF)
+                partial_start(pd, z)
+
+            if pd > 0:
+                partial_pass(pd - 1, j)
             return carry
 
         r["own"][pd] = feed(zi)
@@ -563,12 +634,30 @@
     for pd in range(pds):
         coarse_feed(pd)
 
-    def finish(pd, carry):
-        value = r["mid"][pd].astype(F32) + r["own"][pd]
-        for k in range(1, nz):
-            z = lax.rem(zi + k, nz)
-            partial_from(pd, z).wait_recv()
-            value += T[pd, z].astype(F32)
+    def pass_last(j, carry):
+        partial_pass(pds - 1, j)
+        return carry
+
+    lax.fori_loop(0, nz - 1, pass_last, 0)
+
+    def finish(pd):
+        r["sum"][...] = r["mid"][pd].astype(F32) + r["own"][pd]
+        for way in range(3 if nz > 2 and pd == pds - 1 else 2):
+            end = (zi == 0) | (zi == nz - 1)
+
+            @pl.when((zi > 0, zi < nz - 1, end)[way])
+            def _():
+                pltpu.make_async_remote_copy(
+                    Q.at[pd, zi],
+                    T.at[pd, way],
+                    r["rs0"].at[pd, zi],
+                    r["rr0"].at[pd, way],
+                    device_id=(lat, buddy),
+                    device_id_type=MESH,
+                ).wait_recv()
+                r["sum"][...] = r["sum"][...] + T[pd, way].astype(F32)
+
+        value = r["sum"][...]
         state = value.astype(BF)
         r["cstate"][pd] = state
         expanded = dot32(state, r["v_up"][...])
@@ -576,11 +665,10 @@
         for k in range(4):
             at = slice(k * few, (k + 1) * few)
             cut = slice(k * channels, (k + 1) * channels)
-            r["state"][pd, at, :] = r["state"][pd, at, :] + expanded[:, cut]
-        r["blended"][pd] = dot32(r["B2"][...], r["state"][pd].astype(BF)).astype(BF)
-        return carry
-
-    lax.fori_loop(0, pds, finish, 0)
+            r["blended"][pd, at, :] = (r["state"][pd, at, :] + expanded[:, cut]).astype(BF)
+
+    for pd in range(pds):
+        finish(pd)
 
     for pd in range(pds):
         for cps in halo_copies + back_copies:
@@ -591,7 +679,7 @@
         gather1_drain(pd)
         gather2_drain(pd)
         for k in range(1, nz):
-            partial_to(pd, lax.rem(zi + k, nz)).wait_send()
+            partial(pd, lax.rem(zi + k, nz))[1].wait_send()
         for k in range(n - 1):
             spread_here.one(pd, k).wait_send()
         for k in range(n):
@@ -644,8 +732,7 @@
     fewp = up_to(few, 16)
     hal = up_to(HALO * WD * hc, 16)
 
-    x = fine_field.reshape(pds, WD, rows, cols, channels).transpose(0, 2, 1, 3, 4)
-    x = x.reshape(pds, rows, seg, channels)
+    x = fine_field.transpose(1, 2, 0, 3)
     vmem = pl.BlockSpec(memory_space=pltpu.VMEM)
     hbm = pl.BlockSpec(memory_space=pl.ANY)
     args = [
@@ -695,7 +782,7 @@
         ("U1", pltpu.VMEM((WT, WT), BF)),
         ("B0", pltpu.VMEM((cells, cells), BF)),
         ("B1", pltpu.VMEM((cells, 2 * cells), BF)),
-        ("B2", pltpu.VMEM((cells, cells), BF)),
+        ("v_x", pltpu.VMEM(x.shape, BF)),
         ("P2", pltpu.VMEM((WT, 4 * fewp + 4 * hal), BF)),
         ("U2", pltpu.VMEM((2 * fewp + 2 * hal, 2 * WT), BF)),
         ("K1", pltpu.VMEM((rows // WL, WT, WT), F32)),
@@ -719,7 +806,10 @@
         ("Z", pltpu.VMEM((pds, nz, few, wide), BF)),
         ("own", pltpu.VMEM((pds, few, wide), F32)),
         ("Q", pltpu.VMEM((pds, nz, few, wide), BF)),
-        ("T", pltpu.VMEM((pds, nz, few, wide), BF)),
+        ("T", pltpu.VMEM((pds, 3, few, wide), BF)),
+        ("R", pltpu.VMEM((pds, nz, few, wide), BF)),
+        ("part", pltpu.VMEM((pds, nz, few, wide), F32)),
+        ("sum", pltpu.VMEM((few, wide), F32)),
     ]
     for pd in range(pds):
         for name in ("E", "G"):
@@ -736,9 +826,9 @@
         ("as1", "ar1", (pds, 2, nz - 1)),
         ("ds0", "dr0", (pds, n - 1)),
         ("ds1", "dr1", (pds, n)),
-        ("rs0", "rr0", (pds, nz)),
     ):
         scratch += [(s, sem(shape)), (d, sem(shape))]
+    scratch += [("rs0", sem((pds, nz))), ("rr0", sem((pds, 3))), ("rr1", sem((pds, nz)))]
 
     cfg = dict(m=m, n=n, pds=pds, rows=rows, cols=cols, heads1=heads1, heads2=heads2, hd=hd)
     names = [a[0] for a in args] + [o[0] for o in outs] + [s[0] for s in scratch]
@@ -752,12 +842,16 @@
             collective_id=0, has_side_effects=True, vmem_limit_bytes=63 << 20
         ),
     )(*[a[1] for a in args])
-    blended = blended.reshape(pds, rows, WD, cols, channels).transpose(0, 2, 1, 3, 4)
-    state = state.reshape(pds, half, WD, hc, wide).transpose(0, 2, 1, 3, 4)
-    return (
-        blended.reshape(levels, rows, cols, channels),
-        state.reshape(levels, half, hc, wide),
-    )
+    blended, state = pl.pallas_call(
+        arrange_kernel,
+        out_shape=[
+            jax.ShapeDtypeStruct(x.shape, BF),
+            jax.ShapeDtypeStruct((half, hc, levels, wide), BF),
+        ],
+        in_specs=[vmem, vmem],
+        out_specs=[vmem, vmem],
+    )(blended, state)
+    return blended.transpose(2, 0, 1, 3), state.transpose(2, 0, 1, 3)
 
 
 def solution(mesh):

time: 134 us -> 121 us (0.903)
  local copies, waits for them, and re-layouts: 7.97 us -> 0 us
  Pallas kernels: 125 us -> 120 us
    pallas_call x1, Pallas kernels: 125 us -> 118 us  [body(): pl.pallas_call(functools.partial(step_kernel, cfg, names), out_shape=[o[1...]
    reshape x5 -> x0, local copies, waits for them, and re-layouts: 5.17 us -> none  [the longest x2 2.43 us: body(): fine_field.reshape(pds, WD, rows, cols, channels).transpose(0, 2, 1, 3, 4)]
    pallas_call x0 -> x1, Pallas kernels: none -> 2.75 us  [body(): pl.pallas_call(arrange_kernel, out_shape=[jax.ShapeDtypeStruct(x.shape, B...]
    pallas_call x2 -> x0, local copies, waits for them, and re-layouts: 2.02 us -> none  [body(): pl.pallas_call(functools.partial(step_kernel, cfg, names), out_shape=[o[1...]
where the time goes in v3:
time: 121 us
  Pallas kernels  120 us (99%)
    pallas_call x1, Pallas kernels, body(): pl.pallas_call(functools.partial(step_kernel, cfg, names), out_shape=[o[1...  118 us
    pallas_call x1, Pallas kernels, body(): pl.pallas_call(arrange_kernel, out_shape=[jax.ShapeDtypeStruct(x.shape, B...  2.75 us

profile of v3, /device:TPU:0, one launch (start us, length us, event | category | flops | bytes accessed | tf_op | source)
XLA Modules:
  0.0 120.9 jit_solution(9675454516602386475)
XLA Ops:
  0.6 117.5 %shard_map.194 = (bf16[2,288,512]{2,1,0:T(8,128)(2,1)}, bf16[2,72,1024]{2,1,0:T(8,128)(2,1)}) custom-call(s32[4]{0:T(128)} %refs_0_.1, bf16[12,12,4,512]{3,2,1,0:T(4,128)(2,1)} %bitcast.9, f32[1,512]{1,0:T(1,128)} %bitcast.14, bf16[512,1536]{1,0:T(8,128)(2,1)} %refs_3_.1, f32[16,144,144]{2,1,0:T(8,128)} %refs_4_.1, bf16[512,512]{1,0:T(8,128)(2,1)} %refs_5_.1, ...), custom_call_target="tpu_custom_call" | custom-call | tf_op jit(solution)/shard_map/pallas_call | solution.py:835
  118.1 2.8 %shard_map.195 = (bf16[12,12,4,512]{3,2,1,0:T(4,128)(2,1)}, bf16[6,6,4,1024]{3,2,1,0:T(4,128)(2,1)}) custom-call(bf16[2,288,512]{2,1,0:T(8,128)(2,1)} %get-tuple-element.6.fine_ref, bf16[2,72,1024]{2,1,0:T(8,128)(2,1)} %get-tuple-element.7.coarse_ref), custom_call_target="tpu_custom_call" | custom-call | tf_op jit(solution)/shard_map/pallas_call | solution.py:845

commit v4 on v3

--- a/solution.py
+++ b/solution.py
@@ -326,7 +326,7 @@
         def _():
             final.start()
 
-        straight = nz > 2 and pd == pds - 1
+        straight = nz > 2
 
         @pl.when((reach > 1) & (reach < (nz - 1 if straight else nz)))
         def _():
@@ -341,7 +341,7 @@
     def adds(pd, z):
         first = ((z == 0) & (zi == nz - 2)) | ((z == nz - 1) & (zi == 1))
         inner = (zi > 0) & (zi < nz - 1)
-        return inner & jnp.logical_not(first) if pd == pds - 1 else inner
+        return inner & jnp.logical_not(first)
 
     def partial_pass(pd, j):
         above, below = nz - 1 - zi, zi
@@ -383,6 +383,17 @@
         swap(k).start()
     for key in ("we2", "wr2", "wt2", "wo1", "we1", "wr1", "mw", "b2", "up"):
         loads[key].start()
+
+    def both_streams(step):
+        step(0, 0)
+
+        def pair_of_steps(t, carry):
+            step(0, t)
+            step(1, t - 1)
+            return carry
+
+        lax.fori_loop(1, nz - 1, pair_of_steps, 0)
+        step(1, nz - 2)
 
     def place(index):
         return index // (WL * WW), (index // WW) % WL, index % WW
@@ -517,24 +528,17 @@
         for z in range(nz):
             Y[pd, core, z, few:] = pad
 
-    def coarse_project(pd):
-        def project(z):
-            given = X[pd, z]
-            S[pd, z, pl.ds(0, few)] = dot32(given, r["wt2_o"][1 - core]).astype(BF)
-            cross[0].one(pd, z).start()
-            cross[2].one(pd, z).start()
-            Y[pd, core, z, pl.ds(0, few)] = dot32(given, r["wt2_o"][core]).astype(BF)
-            cross[1].one(pd, z).start()
-
-        def one_chunk(j, carry):
-            project(gather1_arrive(pd, j))
-            return carry
-
-        project(zi)
-        lax.fori_loop(0, nz - 1, one_chunk, 0)
-
-    for pd in range(pds):
-        coarse_project(pd)
+    def project(pd, z):
+        given = X[pd, z]
+        S[pd, z, pl.ds(0, few)] = dot32(given, r["wt2_o"][1 - core]).astype(BF)
+        cross[0].one(pd, z).start()
+        cross[2].one(pd, z).start()
+        Y[pd, core, z, pl.ds(0, few)] = dot32(given, r["wt2_o"][core]).astype(BF)
+        cross[1].one(pd, z).start()
+
+    for pd in range(pds):
+        project(pd, zi)
+    both_streams(lambda pd, j: project(pd, gather1_arrive(pd, j)))
     for k in range(m - 1):
         share_lat.one(k).wait_recv()
     share_core.one(0).start()
@@ -601,48 +605,42 @@
     swap(1).wait_recv()
     swap(2).wait_recv()
 
-    def coarse_feed(pd):
-        def feed(z):
-            given = Z[pd, z]
-            total = None
-            for k in range(2):
-                hidden = jax.nn.gelu(dot32(given, r["v_we2"][k])).astype(BF)
-                term = dot32(hidden, r["v_wr2"][k])
-                total = term if total is None else total + term
-            return total
-
-        def one_chunk(j, carry):
-            z = gather2_arrive(pd, j)
-            term = feed(z)
-
-            @pl.when(adds(pd, z))
-            def _():
-                r["part"][pd, z] = term
-
-            @pl.when(jnp.logical_not(adds(pd, z)))
-            def _():
-                Q[pd, z] = term.astype(BF)
-                partial_start(pd, z)
-
-            if pd > 0:
-                partial_pass(pd - 1, j)
+    def feed(pd, z):
+        given = Z[pd, z]
+        total = None
+        for k in range(2):
+            hidden = jax.nn.gelu(dot32(given, r["v_we2"][k])).astype(BF)
+            term = dot32(hidden, r["v_wr2"][k])
+            total = term if total is None else total + term
+        return total
+
+    def feed_step(pd, j):
+        z = gather2_arrive(pd, j)
+        term = feed(pd, z)
+
+        @pl.when(adds(pd, z))
+        def _():
+            r["part"][pd, z] = term
+
+        @pl.when(jnp.logical_not(adds(pd, z)))
+        def _():
+            Q[pd, z] = term.astype(BF)
+            partial_start(pd, z)
+
+    for pd in range(pds):
+        r["own"][pd] = feed(pd, zi)
+    both_streams(feed_step)
+    for pd in range(pds):
+
+        def pass_one(j, carry):
+            partial_pass(pd, j)
             return carry
 
-        r["own"][pd] = feed(zi)
-        lax.fori_loop(0, nz - 1, one_chunk, 0)
-
-    for pd in range(pds):
-        coarse_feed(pd)
-
-    def pass_last(j, carry):
-        partial_pass(pds - 1, j)
-        return carry
-
-    lax.fori_loop(0, nz - 1, pass_last, 0)
+        lax.fori_loop(0, nz - 1, pass_one, 0)
 
     def finish(pd):
         r["sum"][...] = r["mid"][pd].astype(F32) + r["own"][pd]
-        for way in range(3 if nz > 2 and pd == pds - 1 else 2):
+        for way in range(3 if nz > 2 else 2):
             end = (zi == 0) | (zi == nz - 1)
 
             @pl.when((zi > 0, zi < nz - 1, end)[way])

time: 121 us -> 118 us (0.975)
  Pallas kernels: 120 us -> 117 us
    pallas_call x1, Pallas kernels: 118 us -> 114 us  [body(): pl.pallas_call(functools.partial(step_kernel, cfg, names), out_shape=[o[1...]
where the time goes in v4:
time: 118 us
  Pallas kernels  117 us (99%)
    pallas_call x1, Pallas kernels, body(): pl.pallas_call(functools.partial(step_kernel, cfg, names), out_shape=[o[1...  114 us
    pallas_call x1, Pallas kernels, body(): pl.pallas_call(arrange_kernel, out_shape=[jax.ShapeDtypeStruct(x.shape, B...  2.75 us

profile of v4, /device:TPU:0, one launch (start us, length us, event | category | flops | bytes accessed | tf_op | source)
XLA Modules:
  0.0 117.5 jit_solution(16512224516453028120)
XLA Ops:
  0.6 114.1 %shard_map.194 = (bf16[2,288,512]{2,1,0:T(8,128)(2,1)}, bf16[2,72,1024]{2,1,0:T(8,128)(2,1)}) custom-call(s32[4]{0:T(128)} %refs_0_.1, bf16[12,12,4,512]{3,2,1,0:T(4,128)(2,1)} %bitcast.9, f32[1,512]{1,0:T(1,128)} %bitcast.14, bf16[512,1536]{1,0:T(8,128)(2,1)} %refs_3_.1, f32[16,144,144]{2,1,0:T(8,128)} %refs_4_.1, bf16[512,512]{1,0:T(8,128)(2,1)} %refs_5_.1, ...), custom_call_target="tpu_custom_call" | custom-call | tf_op jit(solution)/shard_map/pallas_call | solution.py:833
  114.7 2.8 %shard_map.195 = (bf16[12,12,4,512]{3,2,1,0:T(4,128)(2,1)}, bf16[6,6,4,1024]{3,2,1,0:T(4,128)(2,1)}) custom-call(bf16[2,288,512]{2,1,0:T(8,128)(2,1)} %get-tuple-element.6.fine_ref, bf16[2,72,1024]{2,1,0:T(8,128)(2,1)} %get-tuple-element.7.coarse_ref), custom_call_target="tpu_custom_call" | custom-call | tf_op jit(solution)/shard_map/pallas_call | solution.py:843

commit v5 on v4

--- a/solution.py
+++ b/solution.py
@@ -374,7 +374,7 @@
             )
     pl.semaphore_wait(barrier, len(greet))
     for pd in range(pds):
-        for cps in halo_copies:
+        for cps in halo_copies[::-1]:
             cps.one(pd).start()
     loads["wo2"].wait()
     for k in range(nz - 1):
@@ -481,7 +481,7 @@
         for k in range(wins):
             turned = dot32(r["U1"][...], r["A"][pl.ds(k * WT, WT), :])
             G[pd][0, pl.ds(HALO + k * WL, WL)] = turned.reshape(WL, seg, -1).astype(BF)
-        for cps in back_copies:
+        for cps in back_copies[::-1]:
             cps.one(pd).start()
 
     for pd in range(pds):
@@ -569,10 +569,10 @@
             return carry
 
         lax.fori_loop(0, nz, one_chip, 0)
+        for k in range(n):
+            spread_next.one(pd, k).start()
         for k in range(n - 1):
             spread_here.one(pd, k).start()
-        for k in range(n):
-            spread_next.one(pd, k).start()
         M[pd, lon] = C[pd, core, zi, pl.ds(0, few)]
         return carry
 

time: 118 us -> 117 us (level)
  Pallas kernels: 117 us -> 115 us
    pallas_call x1, Pallas kernels: 114 us -> 112 us  [body(): pl.pallas_call(functools.partial(step_kernel, cfg, names), out_shape=[o[1...]
where the time goes in v5:
time: 117 us; the launch traced here: 116 us
  Pallas kernels  115 us (98%)
    pallas_call x1, Pallas kernels, body(): pl.pallas_call(functools.partial(step_kernel, cfg, names), out_shape=[o[1...  112 us
    pallas_call x1, Pallas kernels, body(): pl.pallas_call(arrange_kernel, out_shape=[jax.ShapeDtypeStruct(x.shape, B...  2.75 us

profile of v5, /device:TPU:0, one launch (start us, length us, event | category | flops | bytes accessed | tf_op | source)
XLA Modules:
  0.0 115.7 jit_solution(9119096591954595413)
XLA Ops:
  0.6 112.3 %shard_map.194 = (bf16[2,288,512]{2,1,0:T(8,128)(2,1)}, bf16[2,72,1024]{2,1,0:T(8,128)(2,1)}) custom-call(s32[4]{0:T(128)} %refs_0_.1, bf16[12,12,4,512]{3,2,1,0:T(4,128)(2,1)} %bitcast.9, f32[1,512]{1,0:T(1,128)} %bitcast.14, bf16[512,1536]{1,0:T(8,128)(2,1)} %refs_3_.1, f32[16,144,144]{2,1,0:T(8,128)} %refs_4_.1, bf16[512,512]{1,0:T(8,128)(2,1)} %refs_5_.1, ...), custom_call_target="tpu_custom_call" | custom-call | tf_op jit(solution)/shard_map/pallas_call | solution.py:833
  112.9 2.8 %shard_map.195 = (bf16[12,12,4,512]{3,2,1,0:T(4,128)(2,1)}, bf16[6,6,4,1024]{3,2,1,0:T(4,128)(2,1)}) custom-call(bf16[2,288,512]{2,1,0:T(8,128)(2,1)} %get-tuple-element.6.fine_ref, bf16[2,72,1024]{2,1,0:T(8,128)(2,1)} %get-tuple-element.7.coarse_ref), custom_call_target="tpu_custom_call" | custom-call | tf_op jit(solution)/shard_map/pallas_call | solution.py:843
